TPU v7x, 256 devices: a whole 4x4x8 slice. The times are simulated.
256 devices in a mesh: ctx: 32 (over y, z), head: 8 (over x, core).
Axes of the slice: x: 4, y: 4, z: 8, core: 2. Of those that a mesh axis runs over, the one named last changes fastest.
Arguments:
- mixer_input: bfloat16 [32768, 8192], P(('ctx', 'head')), may hold values from -0.0625 to 0.0625
- write_vectors: bfloat16 [32768, 1024], P(('ctx', 'head')), may hold values from -0.1875 to 0.1875
- read_vectors: bfloat16 [32768, 1024], P(('ctx', 'head')), may hold values from -0.1875 to 0.1875
- step_sizes: bfloat16 [32768, 128], P(('ctx', 'head')), may hold values from 0.5 to 22937
- fast_rates: float32 [128], replicated, may hold values from 1.5258789e-06 to 0.034
- slow_heads: int32 [64], replicated, may hold values from 0 to 127, as said below
- skip_gains: float32 [128], replicated, may hold values from 0.5 to 1.5
- mixer_grad: bfloat16 [32768, 8192], P(('ctx', 'head')), may hold values from -6 to 6
- queries: bfloat16 [32768, 4096], P(('ctx', 'head')), may hold values from -150 to 150
- attn_keys: bfloat16 [32768, 1024], P(('ctx', 'head')), may hold values from -6 to 6
- attn_values: bfloat16 [32768, 1024], P(('ctx', 'head')), may hold values from -24 to 24
- attn_grad: bfloat16 [32768, 4096], P(('ctx', 'head')), may hold values from -24 to 24
- doc_lengths: int32 [16], replicated, may hold values from 1 to 3072, 32768 in all
Outputs:
- grad_mixer_input: bfloat16 [32768, 8192], P(('ctx', 'head'))
- grad_write: bfloat16 [32768, 1024], P(('ctx', 'head'))
- grad_read: bfloat16 [32768, 1024], P(('ctx', 'head'))
- grad_queries: bfloat16 [32768, 4096], P(('ctx', 'head'))
Inputs may be any that keep to these rules, and one draw needn't show every extreme that they name: `slow_heads`: distinct head numbers.
All inputs are finite; a program needn't handle non-finite values.
Results may differ from a plain program's by a relative error of at most 0.0062.
Values may be sent and summed in bfloat16 or wider, within the bound.
A program may use at most 192 MiB of HBM per device.

v0:
```python
import jax
import jax.numpy as jnp
from jax import lax
from jax.sharding import Mesh
from jax.sharding import PartitionSpec as P

MH = 128
HD = 64
NS = 128
DH = 128
BLOCK = 256
CTX = ("ctx_0", "ctx_1")
CTX_HEAD = ("ctx_0", "ctx_1", "head")


slab_reach = 3


def filled_with(shard, identity):
    return jax.tree.map(
        lambda a, e: jnp.broadcast_to(jnp.asarray(e, a.dtype), a.shape), shard, identity
    )


def entering_2(shard, axes, combine, identity, reverse):
    before = start = filled_with(shard, identity)
    so_far = shard
    for axis in reversed(axes):
        devices, position = (lax.axis_size(axis), lax.axis_index(axis))
        pieces = jax.tree.map(lambda part: lax.all_gather(part, axis), so_far)
        inside, so_far = (start, start)
        for k in reversed(range(devices)) if reverse else range(devices):
            passed = k > position if reverse else k < position
            so_far = combine(so_far, jax.tree.map(lambda part: part[k], pieces))
            inside = jax.tree.map(lambda new, old: jnp.where(passed, new, old), so_far, inside)
        before = combine(inside, before)
    return before


def from_behind(value, axis, steps):
    count = lax.axis_size(axis)
    leading, last = (max(0, -steps), min(count, count - steps))
    return lax.ppermute(value, axis, [(source, source + steps) for source in range(leading, last)])


def doc_index(positions, doc_lengths):
    starts = jnp.cumsum(doc_lengths) - doc_lengths
    match_count = (starts[None, :] <= positions[:, None]).astype(jnp.int32)
    return jnp.sum(match_count, axis=1) - 1


def combine(earlier, latter):
    factor = latter[0]
    return (earlier[0] * factor, factor[..., None, None] * earlier[1] + latter[1])


def stretch_edges(
    stretch_inputs, stretch_write, stretch_read, decay_log, stretch_grads, docs, doc_prev
):
    cumulative = jnp.cumsum(decay_log, axis=1)
    totals = cumulative[:, -1]
    linked = (docs == doc_prev[:, None]).astype(jnp.float32)
    tail_doc = (docs == docs[:, -1:]).astype(jnp.float32)
    stretch_links = jnp.exp(totals) * linked[:, -1][:, None, None]
    entering = jnp.exp(cumulative) * linked[:, :, None, None]
    to_end = jnp.exp(totals[:, None] - cumulative) * tail_doc[:, :, None, None]
    input_weighted = (stretch_inputs.astype(jnp.float32) * to_end[..., None]).astype(jnp.bfloat16)
    grad_weighted = (stretch_grads.astype(jnp.float32) * entering[..., None]).astype(jnp.bfloat16)
    endings = jnp.einsum(
        "ksghp,ksgn->kghpn", input_weighted, stretch_write, preferred_element_type=jnp.float32
    )
    openings = jnp.einsum(
        "ktghp,ktgn->kghpn", grad_weighted, stretch_read, preferred_element_type=jnp.float32
    )
    return (cumulative, stretch_links, to_end, input_weighted, grad_weighted, endings, openings)


def stretch_inner(stretch_inputs, stretch_write, stretch_read, stretch_grads, docs, cumulative):
    block_rows = stretch_inputs.shape[1]
    offsets = jnp.arange(block_rows, dtype=jnp.int32)
    causal = offsets[:, None] >= offsets[None, :]
    same_doc = causal[None] & (docs[:, :, None] == docs[:, None, :])
    cum_heads = jnp.transpose(cumulative, (0, 2, 3, 1))
    log_gaps = cum_heads[..., :, None] - cum_heads[..., None, :]
    decays = jnp.exp(jnp.where(same_doc[:, None, None], log_gaps, -jnp.inf))
    scores = jnp.einsum(
        "ktgn,ksgn->kgts", stretch_read, stretch_write, preferred_element_type=jnp.float32
    )
    mixing = (scores[:, :, None] * decays).astype(jnp.bfloat16)
    input_inner = jnp.einsum(
        "kghts,ktghp->ksghp", mixing, stretch_grads, preferred_element_type=jnp.float32
    )
    inner_products = jnp.einsum(
        "ktghp,ksghp->kghts", stretch_grads, stretch_inputs, preferred_element_type=jnp.float32
    )
    joint_weights = jnp.sum(inner_products * decays, axis=2).astype(jnp.bfloat16)
    read_inner = jnp.einsum(
        "kgts,ksgn->ktgn", joint_weights, stretch_write, preferred_element_type=jnp.float32
    )
    write_inner = jnp.einsum(
        "kgts,ktgn->ksgn", joint_weights, stretch_read, preferred_element_type=jnp.float32
    )
    return (input_inner, write_inner, read_inner)


def mixer_grads(
    inputs_here,
    write_here,
    read_here,
    steps_here,
    grad_here,
    fast_rates,
    slow_heads,
    skip_gains,
    doc_lengths,
    first_row,
    head_index,
    total_rows,
):
    row_count = inputs_here.shape[0]
    local_heads = steps_here.shape[1]
    local_groups = write_here.shape[1] // NS
    per_group = local_heads // local_groups
    stretch_count = row_count // BLOCK
    head_ids = jnp.arange(MH, dtype=jnp.int32)
    slow_mask = jnp.any(head_ids[:, None] == slow_heads[None, :], axis=1)
    rates = jnp.where(slow_mask, 1.0 / total_rows, fast_rates)
    head_start = head_index * local_heads
    rates_here = lax.dynamic_slice_in_dim(rates, head_start, local_heads).reshape(
        local_groups, per_group
    )
    skips_here = lax.dynamic_slice_in_dim(skip_gains, head_start, local_heads).reshape(
        local_groups, per_group
    )
    decay_log = (
        -steps_here.astype(jnp.float32).reshape(stretch_count, BLOCK, local_groups, per_group)
        * rates_here
    )
    shape_x = (stretch_count, BLOCK, local_groups, per_group, HD)
    shape_v = (stretch_count, BLOCK, local_groups, NS)
    stretch_inputs = inputs_here.reshape(shape_x)
    stretch_grads = grad_here.reshape(shape_x)
    stretch_write = write_here.reshape(shape_v)
    stretch_read = read_here.reshape(shape_v)
    positions = first_row + jnp.arange(row_count, dtype=jnp.int32)
    docs = doc_index(positions, doc_lengths).reshape(stretch_count, BLOCK)
    doc_prev = doc_index(
        first_row - 1 + BLOCK * jnp.arange(stretch_count, dtype=jnp.int32), doc_lengths
    )
    cumulative, stretch_links, to_end, input_weighted, grad_weighted, endings, openings = (
        stretch_edges(
            stretch_inputs, stretch_write, stretch_read, decay_log, stretch_grads, docs, doc_prev
        )
    )
    input_inner, write_inner, read_inner = stretch_inner(
        stretch_inputs, stretch_write, stretch_read, stretch_grads, docs, cumulative
    )

    def forward_local(carried, element):
        stretch_link, ending = element
        return (
            (stretch_link[..., None, None] * carried[0] + ending, stretch_link * carried[1]),
            carried,
        )

    def backward_local(carried, element):
        stretch_link, opening = element
        return (
            (opening + stretch_link[..., None, None] * carried[0], stretch_link * carried[1]),
            carried,
        )

    zero_state = jnp.zeros_like(endings[0])
    unit_links = jnp.ones_like(stretch_links[0])
    (device_end, device_link), (local_states, local_links) = lax.scan(
        forward_local, (zero_state, unit_links), (stretch_links, endings)
    )
    (device_open, unused), (local_backs, back_links) = lax.scan(
        backward_local, (zero_state, unit_links), (stretch_links, openings), reverse=True
    )
    state_in = entering_2((device_link, device_end), CTX, combine, (unit_links, zero_state), False)[
        1
    ]
    back_out = entering_2((device_link, device_open), CTX, combine, (unit_links, zero_state), True)[
        1
    ]
    states_low = (local_states + local_links[..., None, None] * state_in).astype(jnp.bfloat16)
    backs_low = (local_backs + back_links[..., None, None] * back_out).astype(jnp.bfloat16)
    read_carried = jnp.einsum(
        "ktghp,kghpn->ktgn", grad_weighted, states_low, preferred_element_type=jnp.float32
    )
    write_carried = jnp.einsum(
        "ksghp,kghpn->ksgn", input_weighted, backs_low, preferred_element_type=jnp.float32
    )
    input_carried = to_end[..., None] * jnp.einsum(
        "ksgn,kghpn->ksghp", stretch_write, backs_low, preferred_element_type=jnp.float32
    )
    grad_input = (
        input_inner + input_carried + skips_here[..., None] * stretch_grads.astype(jnp.float32)
    ).astype(jnp.bfloat16)
    grad_write = (write_inner + write_carried).astype(jnp.bfloat16)
    grad_read = (read_inner + read_carried).astype(jnp.bfloat16)
    return (
        grad_input.reshape(row_count, -1),
        grad_write.reshape(row_count, -1),
        grad_read.reshape(row_count, -1),
    )


def attend_block(
    query_block, grad_block, key_block, value_block, query_pos, key_pos, query_doc, key_doc
):
    scaling = query_block.shape[-1] ** (-0.5)
    logits = (
        jnp.einsum("qrd,kd->rqk", query_block, key_block, preferred_element_type=jnp.float32)
        * scaling
    )
    allowed = (
        (key_pos[None, :] <= query_pos[:, None])
        & (key_pos[None, :] >= 0)
        & (query_doc[:, None] == key_doc[None, :])
    )
    logits = jnp.where(allowed, logits, -jnp.inf)
    row_peaks = jnp.max(logits, axis=-1, keepdims=True)
    weights = jnp.exp(logits - row_peaks)
    probabilities = weights / jnp.sum(weights, axis=-1, keepdims=True)
    grad_probs = jnp.einsum(
        "qrd,kd->rqk", grad_block, value_block, preferred_element_type=jnp.float32
    )
    centre = jnp.sum(probabilities * grad_probs, axis=-1, keepdims=True)
    grad_logits = (probabilities * (grad_probs - centre)).astype(jnp.bfloat16)
    return (
        jnp.einsum("rqk,kd->qrd", grad_logits, key_block, preferred_element_type=jnp.float32)
        * scaling
    )


def attend(
    query_rows, grad_rows, key_rows, value_rows, first_row, lead_rows, doc_reach, doc_lengths
):
    row_count = query_rows.shape[0]
    kv_heads = key_rows.shape[1] // DH
    group_size = query_rows.shape[1] // key_rows.shape[1]
    query_four = query_rows.reshape(row_count, kv_heads, group_size, DH)
    grad_four = grad_rows.reshape(row_count, kv_heads, group_size, DH)
    key_three = key_rows.reshape(-1, kv_heads, DH)
    value_three = value_rows.reshape(-1, kv_heads, DH)
    block_rows = min(128, row_count)
    block_count = row_count // block_rows
    span = doc_reach + block_rows
    query_positions = first_row + jnp.arange(row_count, dtype=jnp.int32)
    key_positions = first_row - lead_rows + jnp.arange(key_rows.shape[0], dtype=jnp.int32)
    query_docs = doc_index(query_positions, doc_lengths)
    key_docs = doc_index(key_positions, doc_lengths)

    def one_item(index):
        block = index // kv_heads
        which = index % kv_heads
        begin = block * block_rows
        key_begin = begin + lead_rows - doc_reach
        query_part = lax.dynamic_index_in_dim(
            lax.dynamic_slice_in_dim(query_four, begin, block_rows, 0), which, 1, keepdims=False
        )
        grad_part = lax.dynamic_index_in_dim(
            lax.dynamic_slice_in_dim(grad_four, begin, block_rows, 0), which, 1, keepdims=False
        )
        key_part = lax.dynamic_index_in_dim(
            lax.dynamic_slice_in_dim(key_three, key_begin, span, 0), which, 1, keepdims=False
        )
        value_part = lax.dynamic_index_in_dim(
            lax.dynamic_slice_in_dim(value_three, key_begin, span, 0), which, 1, keepdims=False
        )
        return attend_block(
            query_part,
            grad_part,
            key_part,
            value_part,
            lax.dynamic_slice_in_dim(query_positions, begin, block_rows, 0),
            lax.dynamic_slice_in_dim(key_positions, key_begin, span, 0),
            lax.dynamic_slice_in_dim(query_docs, begin, block_rows, 0),
            lax.dynamic_slice_in_dim(key_docs, key_begin, span, 0),
        )

    items = lax.map(one_item, jnp.arange(block_count * kv_heads, dtype=jnp.int32))
    items = items.reshape(block_count, kv_heads, block_rows, group_size, DH).transpose(
        0, 2, 1, 3, 4
    )
    return items.reshape(row_count, -1).astype(jnp.bfloat16)


def head_attention(query_rows, key_rows, value_rows, grad_rows, doc_lengths, first_row):
    row_count = query_rows.shape[0]
    earlier_keys = []
    earlier_values = []
    for distance in range(slab_reach, 0, -1):
        fetched = from_behind((key_rows, value_rows), CTX, distance)
        earlier_keys.append(fetched[0])
        earlier_values.append(fetched[1])
    key_all = jnp.concatenate(earlier_keys + [key_rows], axis=0)
    value_all = jnp.concatenate(earlier_values + [value_rows], axis=0)
    lead = slab_reach * row_count
    return attend(query_rows, grad_rows, key_all, value_all, first_row, lead, lead, doc_lengths)


def shards(
    mixer_input,
    write_vectors,
    read_vectors,
    step_sizes,
    fast_rates,
    slow_heads,
    skip_gains,
    mixer_grad,
    queries,
    attn_keys,
    attn_values,
    attn_grad,
    doc_lengths,
):
    head_count = lax.axis_size("head")
    ctx_index = lax.axis_index(CTX)
    head_index = lax.axis_index("head")
    shard_rows = mixer_input.shape[0] * head_count
    total_rows = shard_rows * lax.axis_size(CTX)
    moved = (
        lax.all_to_all(mixer_input, "head", split_axis=1, concat_axis=0, tiled=True),
        lax.all_to_all(write_vectors, "head", split_axis=1, concat_axis=0, tiled=True),
        lax.all_to_all(read_vectors, "head", split_axis=1, concat_axis=0, tiled=True),
        lax.all_to_all(step_sizes, "head", split_axis=1, concat_axis=0, tiled=True),
        lax.all_to_all(mixer_grad, "head", split_axis=1, concat_axis=0, tiled=True),
        lax.all_to_all(queries, "head", split_axis=1, concat_axis=0, tiled=True),
        lax.all_to_all(attn_keys, "head", split_axis=1, concat_axis=0, tiled=True),
        lax.all_to_all(attn_values, "head", split_axis=1, concat_axis=0, tiled=True),
        lax.all_to_all(attn_grad, "head", split_axis=1, concat_axis=0, tiled=True),
    )
    grad_query_heads = head_attention(
        moved[5], moved[6], moved[7], moved[8], doc_lengths, ctx_index * shard_rows
    )
    grad_input, grad_write, grad_read = mixer_grads(
        moved[0],
        moved[1],
        moved[2],
        moved[3],
        moved[4],
        fast_rates,
        slow_heads,
        skip_gains,
        doc_lengths,
        ctx_index * shard_rows,
        head_index,
        total_rows,
    )
    returned = (
        lax.all_to_all(grad_input, "head", split_axis=0, concat_axis=1, tiled=True),
        lax.all_to_all(grad_write, "head", split_axis=0, concat_axis=1, tiled=True),
        lax.all_to_all(grad_read, "head", split_axis=0, concat_axis=1, tiled=True),
        lax.all_to_all(grad_query_heads, "head", split_axis=0, concat_axis=1, tiled=True),
    )
    return (returned[0], returned[1], returned[2], returned[3])


def solution(mesh):
    split = Mesh(mesh.devices.reshape(4, 8, mesh.shape["head"]), ("ctx_0", "ctx_1", "head"))
    return jax.shard_map(
        shards,
        mesh=split,
        in_specs=(
            P(CTX_HEAD, None),
            P(CTX_HEAD, None),
            P(CTX_HEAD, None),
            P(CTX_HEAD, None),
            P(),
            P(),
            P(),
            P(CTX_HEAD, None),
            P(CTX_HEAD, None),
            P(CTX_HEAD, None),
            P(CTX_HEAD, None),
            P(CTX_HEAD, None),
            P(),
        ),
        out_specs=(P(CTX_HEAD, None), P(CTX_HEAD, None), P(CTX_HEAD, None), P(CTX_HEAD, None)),
        check_vma=False,
    )
```

profile of v0, /device:TPU:1, one launch (start us, length us, event | category | flops | bytes accessed | tf_op | source)
XLA Modules:
  0.0 617.0 jit_solution(6818892694384859744)
XLA Ops:
  8.7 6.5 %all-to-all-start.2 = ((bf16[128,8,16]{0,2,1:T(8,128)(2,1)}), bf16[128,8,16]{0,2,1:T(8,128)(2,1)S(1)}, u32[]{:S(2)}, u32[]{:S(2)}) async-start(bf16[128,8,16]{0,2,1:T(8,128)(2,1)} %bitcast.17), calls=%async_computation.2 | async-start | bytes 65536 | tf_op jit(solution)/shard_map/all_to_all | solution.py:329
  18.8 4.1 copy.247
  22.9 5.0 all-to-all-start.4
  32.0 22.2 %all-to-all-done.4 = bf16[128,8,1024]{0,2,1:T(8,128)(2,1)S(1)} async-done(((bf16[128,8,1024]{0,2,1:T(8,128)(2,1)}), bf16[128,8,1024]{0,2,1:T(8,128)(2,1)S(1)}, u32[]{:S(2)}, u32[]{:S(2)}) %all-to-all-start.4) | async-done | bytes 2097184 | tf_op jit(solution)/shard_map/all_to_all | solution.py:326
  54.2 4.2 all-to-all-start.1
  61.0 4.4 reshape.901
  70.4 5.2 while.54
  76.4 4.1 copy.239
  80.5 5.0 all-to-all-start.3
  86.3 25.5 %all-to-all-done.3 = bf16[128,8,1024]{0,2,1:T(8,128)(2,1)S(1)} async-done(((bf16[128,8,1024]{0,2,1:T(8,128)(2,1)}), bf16[128,8,1024]{0,2,1:T(8,128)(2,1)S(1)}, u32[]{:S(2)}, u32[]{:S(2)}) %all-to-all-start.3) | async-done | bytes 2097184 | tf_op jit(solution)/shard_map/all_to_all | solution.py:330
  111.8 4.2 all-to-all-start
  118.7 4.4 reshape.898
  129.3 8.2 %while.53 = (s32[]{:T(128)}, f32[1,16,64,128]{3,2,1,0:T(8,128)S(1)}, f32[1,16]{1,0:T(1,128)S(1)}, f32[4,1,16,64,128]{4,3,2,1,0:T(8,128)}, f32[4,1,16]{2,1,0:T(1,...) while((s32[]{:T(128)}, ...), condition=%wide.region_7.8_spmd.clone, body=%wide.region_6.7_spmd.clone.sunk | while | flops 524340 | bytes 2622994 | solution.py:178
  138.4 14.6 %all-gather.3 = f32[8,1,16]{2,1,0:T(1,128)S(1)} all-gather(f32[1,1,16]{2,1,0:T(1,128)S(1)} %bitcast.562), channel_id=2, replica_groups=mesh['ctx_0'=4,'ctx_1'=8,'head'=8] {'ctx_1'}, dimensions={0}, use_global_device_ids=true | all-gather | bytes 576 | tf_op jit(solution)/shard_map/all_gather | solution.py:30
  159.4 8.6 %all-to-all-start.8 = ((bf16[128,8,128]{2,0,1:T(8,128)(2,1)}), bf16[128,8,128]{2,0,1:T(8,128)(2,1)}, u32[]{:S(2)}, u32[]{:S(2)}) async-start(bf16[128,8,128]{2,0,1:T(8,128)(2,1)} %copy_bitcast_fusion.3), calls=%async_computation.8 | async-start | bytes 524288 | tf_op jit(solution)/shard_map/all_to_all | solution.py:332
  169.7 4.9 all-to-all-done.8
  174.6 5.2 all-to-all-start.10
  186.4 4.5 all-to-all-start.9
  200.3 5.0 collective-permute-start.1
  207.4 5.0 collective-permute-start.3
  217.9 6.2 %all-to-all-start.11 = ((bf16[128,8,512]{0,2,1:T(8,128)(2,1)}), bf16[128,8,512]{0,2,1:T(8,128)(2,1)}, u32[]{:S(2)}, u32[]{:S(2)}) async-start(bf16[128,8,512]{0,2,1:T(8,128)(2,1)} %bitcast.111), calls=%async_computation.11 | async-start | bytes 2097152 | tf_op jit(solution)/shard_map/all_to_all | solution.py:334
  227.3 6.4 %collective-permute-done.2 = bf16[1024,128]{1,0:T(8,128)(2,1)} collective-permute-done((bf16[1024,128]{1,0:T(8,128)(2,1)}, bf16[1024,128]{1,0:T(8,128)(2,1)}, u32[]{:S(2)}, u32[]{:S(2)}) %collective-permute-start.2) | collective-permute-done | bytes 262176 | tf_op jit(solution)/shard_map/ppermute | solution.py:43
  236.0 13.2 %collective-permute-done.3 = bf16[1024,128]{1,0:T(8,128)(2,1)} collective-permute-done((bf16[1024,128]{1,0:T(8,128)(2,1)}, bf16[1024,128]{1,0:T(8,128)(2,1)}, u32[]{:S(2)}, u32[]{:S(2)}) %collective-permute-start.3) | collective-permute-done | bytes 262176 | tf_op jit(solution)/shard_map/ppermute | solution.py:43
  249.2 7.6 %collective-permute-done.4 = bf16[1024,128]{1,0:T(8,128)(2,1)} collective-permute-done((bf16[1024,128]{1,0:T(8,128)(2,1)}, bf16[1024,128]{1,0:T(8,128)(2,1)}, u32[]{:S(2)}, u32[]{:S(2)}) %collective-permute-start.4) | collective-permute-done | bytes 262176 | tf_op jit(solution)/shard_map/ppermute | solution.py:43
  256.8 10.6 %collective-permute-done.5 = bf16[1024,128]{1,0:T(8,128)(2,1)S(1)} collective-permute-done((bf16[1024,128]{1,0:T(8,128)(2,1)}, bf16[1024,128]{1,0:T(8,128)(2,1)S(1)}, u32[]{:S(2)}, u32[]{:S(2)}) %collective-permute-start.5) | collective-permute-done | bytes 262176 | tf_op jit(solution)/shard_map/ppermute | solution.py:43
  280.3 198.3 %while.52 = (s32[]{:T(128)}, bf16[8,128,4,128]{1,3,2,0:T(8,128)(2,1)}, s32[8]{0:T(128)S(1)}, bf16[4096,1,128]{2,0,1:T(8,128)(2,1)}, s32[4096]{0:T(1024)S(1)}, /*...) while((s32[]{:T(128)}, ...), condition=%wide.region_16.17_spmd, body=%wide.region_12.16_spmd.sunk | while | flops 1702372736 | bytes 31474184 | solution.py:284
  284.7 5.9 fusion.181
  290.6 7.1 %fusion.182 = (f32[4,128]{1,0:T(4,128)S(1)}, f32[3200,128,4]{1,0,2:T(8,128)}) fusion(f32[4,128,3200]{1,2,0:T(8,128)} %get-tuple-element.851, f32[4,128]{1,0:T(4,128)S(1)} %get-tuple-element.852, bf16[1024,1,4,128]{0,3,2,1:T(8,128)(2,1)} %get-tuple-element.968, s32[]{:T(128)S(6)} %select_n.734, bf16[4096,1,128]{2,0,1:T(8,128)(2,1)} %get-tuple-element.967, ...), kind=kOutput, calls=%fused_computation.5.clone.1 | convolution fusion | flops 424345088 | bytes 14061576 | tf_op jit(solution)/shard_map/while/body/eval_jaxpr/qrd,kd->rqk/dot_general | solution.py:227
  297.7 7.6 %fusion.183 = bf16[8,128,4,128]{1,3,2,0:T(8,128)(2,1)} fusion(bf16[8,128,4,128]{1,3,2,0:T(8,128)(2,1)} %get-tuple-element.943, s32[]{:T(128)} %get-tuple-element.942, f32[3200,128,4]{1,0,2:T(8,128)} %get-tuple-element.853, f32[4,128]{1,0:T(4,128)S(1)} %get-tuple-element.854, f32[4,128]{1,0:T(4,128)S(1)} %get-tuple-element.852, ...), kind=kOutput, calls=%fused_computation.16.clone.1 | convolution fusion | flops 850398848 | bytes 9000960 | tf_op jit(solution)/shard_map/while/body/eval_jaxpr/rqk,kd->qrd/dot_general | solution.py:233
  309.7 5.9 fusion.181
  315.6 6.9 %fusion.182 = (f32[4,128]{1,0:T(4,128)S(1)}, f32[3200,128,4]{1,0,2:T(8,128)}) fusion(f32[4,128,3200]{1,2,0:T(8,128)} %get-tuple-element.851, f32[4,128]{1,0:T(4,128)S(1)} %get-tuple-element.852, bf16[1024,1,4,128]{0,3,2,1:T(8,128)(2,1)} %get-tuple-element.968, s32[]{:T(128)S(6)} %select_n.734, bf16[4096,1,128]{2,0,1:T(8,128)(2,1)} %get-tuple-element.967, ...), kind=kOutput, calls=%fused_computation.5.clone.1 | convolution fusion | flops 424345088 | bytes 14061576 | tf_op jit(solution)/shard_map/while/body/eval_jaxpr/qrd,kd->rqk/dot_general | solution.py:227
  322.5 7.5 %fusion.183 = bf16[8,128,4,128]{1,3,2,0:T(8,128)(2,1)} fusion(bf16[8,128,4,128]{1,3,2,0:T(8,128)(2,1)} %get-tuple-element.943, s32[]{:T(128)} %get-tuple-element.942, f32[3200,128,4]{1,0,2:T(8,128)} %get-tuple-element.853, f32[4,128]{1,0:T(4,128)S(1)} %get-tuple-element.854, f32[4,128]{1,0:T(4,128)S(1)} %get-tuple-element.852, ...), kind=kOutput, calls=%fused_computation.16.clone.1 | convolution fusion | flops 850398848 | bytes 9000960 | tf_op jit(solution)/shard_map/while/body/eval_jaxpr/rqk,kd->qrd/dot_general | solution.py:233
  334.4 5.9 fusion.181
  340.3 6.9 %fusion.182 = (f32[4,128]{1,0:T(4,128)S(1)}, f32[3200,128,4]{1,0,2:T(8,128)}) fusion(f32[4,128,3200]{1,2,0:T(8,128)} %get-tuple-element.851, f32[4,128]{1,0:T(4,128)S(1)} %get-tuple-element.852, bf16[1024,1,4,128]{0,3,2,1:T(8,128)(2,1)} %get-tuple-element.968, s32[]{:T(128)S(6)} %select_n.734, bf16[4096,1,128]{2,0,1:T(8,128)(2,1)} %get-tuple-element.967, ...), kind=kOutput, calls=%fused_computation.5.clone.1 | convolution fusion | flops 424345088 | bytes 14061576 | tf_op jit(solution)/shard_map/while/body/eval_jaxpr/qrd,kd->rqk/dot_general | solution.py:227
  347.3 7.5 %fusion.183 = bf16[8,128,4,128]{1,3,2,0:T(8,128)(2,1)} fusion(bf16[8,128,4,128]{1,3,2,0:T(8,128)(2,1)} %get-tuple-element.943, s32[]{:T(128)} %get-tuple-element.942, f32[3200,128,4]{1,0,2:T(8,128)} %get-tuple-element.853, f32[4,128]{1,0:T(4,128)S(1)} %get-tuple-element.854, f32[4,128]{1,0:T(4,128)S(1)} %get-tuple-element.852, ...), kind=kOutput, calls=%fused_computation.16.clone.1 | convolution fusion | flops 850398848 | bytes 9000960 | tf_op jit(solution)/shard_map/while/body/eval_jaxpr/rqk,kd->qrd/dot_general | solution.py:233
  359.2 5.9 fusion.181
  365.1 6.9 %fusion.182 = (f32[4,128]{1,0:T(4,128)S(1)}, f32[3200,128,4]{1,0,2:T(8,128)}) fusion(f32[4,128,3200]{1,2,0:T(8,128)} %get-tuple-element.851, f32[4,128]{1,0:T(4,128)S(1)} %get-tuple-element.852, bf16[1024,1,4,128]{0,3,2,1:T(8,128)(2,1)} %get-tuple-element.968, s32[]{:T(128)S(6)} %select_n.734, bf16[4096,1,128]{2,0,1:T(8,128)(2,1)} %get-tuple-element.967, ...), kind=kOutput, calls=%fused_computation.5.clone.1 | convolution fusion | flops 424345088 | bytes 14061576 | tf_op jit(solution)/shard_map/while/body/eval_jaxpr/qrd,kd->rqk/dot_general | solution.py:227
  372.0 7.5 %fusion.183 = bf16[8,128,4,128]{1,3,2,0:T(8,128)(2,1)} fusion(bf16[8,128,4,128]{1,3,2,0:T(8,128)(2,1)} %get-tuple-element.943, s32[]{:T(128)} %get-tuple-element.942, f32[3200,128,4]{1,0,2:T(8,128)} %get-tuple-element.853, f32[4,128]{1,0:T(4,128)S(1)} %get-tuple-element.854, f32[4,128]{1,0:T(4,128)S(1)} %get-tuple-element.852, ...), kind=kOutput, calls=%fused_computation.16.clone.1 | convolution fusion | flops 850398848 | bytes 9000960 | tf_op jit(solution)/shard_map/while/body/eval_jaxpr/rqk,kd->qrd/dot_general | solution.py:233
  383.9 5.9 fusion.181
  389.8 6.9 %fusion.182 = (f32[4,128]{1,0:T(4,128)S(1)}, f32[3200,128,4]{1,0,2:T(8,128)}) fusion(f32[4,128,3200]{1,2,0:T(8,128)} %get-tuple-element.851, f32[4,128]{1,0:T(4,128)S(1)} %get-tuple-element.852, bf16[1024,1,4,128]{0,3,2,1:T(8,128)(2,1)} %get-tuple-element.968, s32[]{:T(128)S(6)} %select_n.734, bf16[4096,1,128]{2,0,1:T(8,128)(2,1)} %get-tuple-element.967, ...), kind=kOutput, calls=%fused_computation.5.clone.1 | convolution fusion | flops 424345088 | bytes 14061576 | tf_op jit(solution)/shard_map/while/body/eval_jaxpr/qrd,kd->rqk/dot_general | solution.py:227
  396.8 7.5 %fusion.183 = bf16[8,128,4,128]{1,3,2,0:T(8,128)(2,1)} fusion(bf16[8,128,4,128]{1,3,2,0:T(8,128)(2,1)} %get-tuple-element.943, s32[]{:T(128)} %get-tuple-element.942, f32[3200,128,4]{1,0,2:T(8,128)} %get-tuple-element.853, f32[4,128]{1,0:T(4,128)S(1)} %get-tuple-element.854, f32[4,128]{1,0:T(4,128)S(1)} %get-tuple-element.852, ...), kind=kOutput, calls=%fused_computation.16.clone.1 | convolution fusion | flops 850398848 | bytes 9000960 | tf_op jit(solution)/shard_map/while/body/eval_jaxpr/rqk,kd->qrd/dot_general | solution.py:233
  408.7 5.9 fusion.181
  414.6 6.9 %fusion.182 = (f32[4,128]{1,0:T(4,128)S(1)}, f32[3200,128,4]{1,0,2:T(8,128)}) fusion(f32[4,128,3200]{1,2,0:T(8,128)} %get-tuple-element.851, f32[4,128]{1,0:T(4,128)S(1)} %get-tuple-element.852, bf16[1024,1,4,128]{0,3,2,1:T(8,128)(2,1)} %get-tuple-element.968, s32[]{:T(128)S(6)} %select_n.734, bf16[4096,1,128]{2,0,1:T(8,128)(2,1)} %get-tuple-element.967, ...), kind=kOutput, calls=%fused_computation.5.clone.1 | convolution fusion | flops 424345088 | bytes 14061576 | tf_op jit(solution)/shard_map/while/body/eval_jaxpr/qrd,kd->rqk/dot_general | solution.py:227
  421.5 7.5 %fusion.183 = bf16[8,128,4,128]{1,3,2,0:T(8,128)(2,1)} fusion(bf16[8,128,4,128]{1,3,2,0:T(8,128)(2,1)} %get-tuple-element.943, s32[]{:T(128)} %get-tuple-element.942, f32[3200,128,4]{1,0,2:T(8,128)} %get-tuple-element.853, f32[4,128]{1,0:T(4,128)S(1)} %get-tuple-element.854, f32[4,128]{1,0:T(4,128)S(1)} %get-tuple-element.852, ...), kind=kOutput, calls=%fused_computation.16.clone.1 | convolution fusion | flops 850398848 | bytes 9000960 | tf_op jit(solution)/shard_map/while/body/eval_jaxpr/rqk,kd->qrd/dot_general | solution.py:233
  433.4 5.9 fusion.181
  439.3 6.9 %fusion.182 = (f32[4,128]{1,0:T(4,128)S(1)}, f32[3200,128,4]{1,0,2:T(8,128)}) fusion(f32[4,128,3200]{1,2,0:T(8,128)} %get-tuple-element.851, f32[4,128]{1,0:T(4,128)S(1)} %get-tuple-element.852, bf16[1024,1,4,128]{0,3,2,1:T(8,128)(2,1)} %get-tuple-element.968, s32[]{:T(128)S(6)} %select_n.734, bf16[4096,1,128]{2,0,1:T(8,128)(2,1)} %get-tuple-element.967, ...), kind=kOutput, calls=%fused_computation.5.clone.1 | convolution fusion | flops 424345088 | bytes 14061576 | tf_op jit(solution)/shard_map/while/body/eval_jaxpr/qrd,kd->rqk/dot_general | solution.py:227
  446.3 7.5 %fusion.183 = bf16[8,128,4,128]{1,3,2,0:T(8,128)(2,1)} fusion(bf16[8,128,4,128]{1,3,2,0:T(8,128)(2,1)} %get-tuple-element.943, s32[]{:T(128)} %get-tuple-element.942, f32[3200,128,4]{1,0,2:T(8,128)} %get-tuple-element.853, f32[4,128]{1,0:T(4,128)S(1)} %get-tuple-element.854, f32[4,128]{1,0:T(4,128)S(1)} %get-tuple-element.852, ...), kind=kOutput, calls=%fused_computation.16.clone.1 | convolution fusion | flops 850398848 | bytes 9000960 | tf_op jit(solution)/shard_map/while/body/eval_jaxpr/rqk,kd->qrd/dot_general | solution.py:233
  458.2 5.9 fusion.181
  464.1 6.9 %fusion.182 = (f32[4,128]{1,0:T(4,128)S(1)}, f32[3200,128,4]{1,0,2:T(8,128)}) fusion(f32[4,128,3200]{1,2,0:T(8,128)} %get-tuple-element.851, f32[4,128]{1,0:T(4,128)S(1)} %get-tuple-element.852, bf16[1024,1,4,128]{0,3,2,1:T(8,128)(2,1)} %get-tuple-element.968, s32[]{:T(128)S(6)} %select_n.734, bf16[4096,1,128]{2,0,1:T(8,128)(2,1)} %get-tuple-element.967, ...), kind=kOutput, calls=%fused_computation.5.clone.1 | convolution fusion | flops 424345088 | bytes 14061576 | tf_op jit(solution)/shard_map/while/body/eval_jaxpr/qrd,kd->rqk/dot_general | solution.py:227
  471.0 7.5 %fusion.183 = bf16[8,128,4,128]{1,3,2,0:T(8,128)(2,1)} fusion(bf16[8,128,4,128]{1,3,2,0:T(8,128)(2,1)} %get-tuple-element.943, s32[]{:T(128)} %get-tuple-element.942, f32[3200,128,4]{1,0,2:T(8,128)} %get-tuple-element.853, f32[4,128]{1,0:T(4,128)S(1)} %get-tuple-element.854, f32[4,128]{1,0:T(4,128)S(1)} %get-tuple-element.852, ...), kind=kOutput, calls=%fused_computation.16.clone.1 | convolution fusion | flops 850398848 | bytes 9000960 | tf_op jit(solution)/shard_map/while/body/eval_jaxpr/rqk,kd->qrd/dot_general | solution.py:233
  480.8 5.8 all-to-all-start.12
  488.5 4.5 copy.253
  492.9 5.7 reshape.908
  498.6 11.1 %all_gather.42 = f32[4,1,16]{2,1,0:T(1,128)S(1)} all-gather(f32[1,1,16]{2,1,0:T(1,128)S(1)} %copy-done.31), channel_id=1, replica_groups=mesh['ctx_0'=4,'ctx_1'=8,'head'=8] {'ctx_0'}, dimensions={0}, use_global_device_ids=true | all-gather | bytes 320 | tf_op jit(solution)/shard_map/all_gather | solution.py:30
  509.7 5.2 all_gather.38
  514.9 7.5 %multiply_reduce_fusion = bf16[4,256,256]{2,1,0:T(8,128)(2,1)S(1)} fusion(f32[4,16,256]{2,1,0:T(8,128)S(1)} %copy-done.23, pred[4,256,256]{2,1,0:T(8,128)(4,1)} %compare_and_fusion.1, bf16[4,256,16,64]{1,0,3,2:T(4,128)(2,1)} %reshape.901, bf16[4,256,16,64]{1,0,3,2:T(4,128)(2,1)} %reshape.898), kind=kOutput, calls=%fused_computation.56 | convolution fusion | flops 553385984 | bytes 5046272 | tf_op jit(solution)/shard_map/ktghp,ksghp->kghts/dot_general | solution.py:93
  522.5 4.0 fusion.109
  528.4 4.0 fusion.121
  538.1 8.7 %all-to-all-start.7 = ((bf16[8,128,128]{2,1,0:T(8,128)(2,1)}), bf16[8,128,128]{2,1,0:T(8,128)(2,1)S(1)}, u32[]{:S(2)}, u32[]{:S(2)}) async-start(bf16[8,128,128]{2,1,0:T(8,128)(2,1)} %bitcast.99), calls=%async_computation.7 | async-start | bytes 524288 | tf_op jit(solution)/shard_map/all_to_all | solution.py:356
  548.9 4.4 all-to-all-done.7
  553.3 4.6 all-to-all-start.6
  558.0 10.0 %fusion.73 = bf16[4,256,1,16,64]{1,4,3,0,2:T(8,128)(2,1)S(1)} fusion(f32[4,16,64,256]{3,2,1,0:T(8,128)} %fusion.134, f32[4,256,1,16,64]{1,0,4,3,2:T(4,128)} %reshape.908, f32[4,16,256]{2,1,0:T(8,128)S(1)} %copy-done.24, f32[4,256,256]{2,1,0:T(8,128)} %fusion.148, pred[4,256,256]{2,1,0:T(8,128)(4,1)S(1)} %copy-done.20, f32[16]{0:T(128)S(1)} %copy-done.34, ...), kind=kOutput, calls=%fused_computation.68 | convolution fusion | flops 558891008 | bytes 14024768 | tf_op jit(solution)/shard_map/kghts,ktghp->ksghp/dot_general | solution.py:90
  575.9 4.8 all-to-all-start.5
  586.1 21.0 %all-to-all-done.5 = bf16[8,128,1024]{1,2,0:T(8,128)(2,1)S(1)} async-done(((bf16[8,128,1024]{1,2,0:T(8,128)(2,1)}), bf16[8,128,1024]{1,2,0:T(8,128)(2,1)S(1)}, u32[]{:S(2)}, u32[]{:S(2)}) %all-to-all-start.5) | async-done | bytes 2097184 | tf_op jit(solution)/shard_map/all_to_all | solution.py:354
  (285 shorter events, 150.9 us)
Async XLA Ops:
  7.2 10.1 %copy-start = (bf16[128,1024]{1,0:T(8,128)(2,1)S(1)}, bf16[128,1024]{1,0:T(8,128)(2,1)}, u32[]{:S(2)}) copy-start(bf16[128,1024]{1,0:T(8,128)(2,1)} %param.20) | copy-start | bytes 786436
  8.7 14.2 %all-to-all-start.2 = ((bf16[128,8,16]{0,2,1:T(8,128)(2,1)}), bf16[128,8,16]{0,2,1:T(8,128)(2,1)S(1)}, u32[]{:S(2)}, u32[]{:S(2)}) async-start(bf16[128,8,16]{0,2,1:T(8,128)(2,1)} %bitcast.17), calls=%async_computation.2 | async-start | bytes 65536 | tf_op jit(solution)/shard_map/all_to_all | solution.py:329
  22.9 5.0 copy-start.32
  22.9 31.3 %all-to-all-start.4 = ((bf16[128,8,1024]{0,2,1:T(8,128)(2,1)}), bf16[128,8,1024]{0,2,1:T(8,128)(2,1)S(1)}, u32[]{:S(2)}, u32[]{:S(2)}) async-start(bf16[128,8,1024]{0,2,1:T(8,128)(2,1)} %bitcast.540), calls=%async_computation.4 | async-start | bytes 4194304 | tf_op jit(solution)/shard_map/all_to_all | solution.py:326
  31.2 23.0 %copy-start.18 = (f32[4,16,2,128]{3,2,1,0:T(2,128)}, f32[4,16,2,128]{3,2,1,0:T(2,128)S(1)}, u32[]{:S(2)}) copy-start(f32[4,16,2,128]{3,2,1,0:T(2,128)S(1)} %broadcast.608) | copy-start | bytes 196612
  31.9 22.3 %copy-start.21 = (f32[4,256,1,16]{1,3,2,0:T(8,128)}, f32[4,256,1,16]{1,3,2,0:T(8,128)S(1)}, u32[]{:S(2)}) copy-start(f32[4,256,1,16]{1,3,2,0:T(8,128)S(1)} %copy.332) | copy-start | bytes 196612
  54.2 13.9 %all-to-all-start.1 = ((bf16[128,8,128]{2,0,1:T(8,128)(2,1)}), bf16[128,8,128]{2,0,1:T(8,128)(2,1)S(1)}, u32[]{:S(2)}, u32[]{:S(2)}) async-start(bf16[128,8,128]{2,0,1:T(8,128)(2,1)} %copy_bitcast_fusion.4), calls=%async_computation.1 | async-start | bytes 524288 | tf_op jit(solution)/shard_map/all_to_all | solution.py:327
  58.4 95.8 %all-gather.15.cloned.1.call-start = ((), (), s32[]{:S(2)}) async-start(), calls=%async_computation.16 | async-start | bytes 4718592 | tf_op jit(solution)/shard_map/all_gather | solution.py:30
  68.1 2.1 copy-start.4
  75.5 0.8 copy-start.2
  75.6 4.9 copy-start.8
  75.6 4.9 copy-start.25
  80.5 5.0 copy-start.19
  80.5 31.3 %all-to-all-start.3 = ((bf16[128,8,1024]{0,2,1:T(8,128)(2,1)}), bf16[128,8,1024]{0,2,1:T(8,128)(2,1)S(1)}, u32[]{:S(2)}, u32[]{:S(2)}) async-start(bf16[128,8,1024]{0,2,1:T(8,128)(2,1)} %bitcast.542), calls=%async_computation.3 | async-start | bytes 4194304 | tf_op jit(solution)/shard_map/all_to_all | solution.py:330
  111.8 6.9 %copy-start.7 = (bf16[128,8,1024]{0,2,1:T(8,128)(2,1)}, bf16[128,8,1024]{0,2,1:T(8,128)(2,1)S(1)}, u32[]{:S(2)}) copy-start(bf16[128,8,1024]{0,2,1:T(8,128)(2,1)S(1)} %all-to-all-done.3) | copy-start | bytes 6291460
  111.8 13.9 %all-to-all-start = ((bf16[128,8,128]{2,0,1:T(8,128)(2,1)}), bf16[128,8,128]{2,0,1:T(8,128)(2,1)S(1)}, u32[]{:S(2)}, u32[]{:S(2)}) async-start(bf16[128,8,128]{2,0,1:T(8,128)(2,1)} %copy_bitcast_fusion.5), calls=%async_computation | async-start | bytes 524288 | tf_op jit(solution)/shard_map/all_to_all | solution.py:328
  116.0 160.7 %all-gather.13.cloned.1.call-start = ((), (), s32[]{:S(2)}) async-start(), calls=%async_computation.15 | async-start | bytes 4718592 | tf_op jit(solution)/shard_map/all_gather | solution.py:30
  125.7 2.0 copy-start.13
  137.6 0.8 copy-start.3
  138.4 384.1 %all-gather.11.cloned.1.call-start = ((), (), s32[]{:S(2)}) async-start(), calls=%async_computation.14 | async-start | bytes 2621440 | tf_op jit(solution)/shard_map/all_gather | solution.py:30
  154.1 3.4 copy-start.27
  157.6 22.3 %copy-start.33 = (f32[128]{0:T(128)S(1)}, f32[128]{0:T(128)}, u32[]{:S(2)}) copy-start(f32[128]{0:T(128)} %param.25) | copy-start | bytes 1540
  157.6 23.0 %copy-start.16 = (bf16[128,4096]{1,0:T(8,128)(2,1)S(1)}, bf16[128,4096]{1,0:T(8,128)(2,1)}, u32[]{:S(2)}) copy-start(bf16[128,4096]{1,0:T(8,128)(2,1)} %param.27) | copy-start | bytes 3145732
  159.4 15.2 %all-to-all-start.8 = ((bf16[128,8,128]{2,0,1:T(8,128)(2,1)}), bf16[128,8,128]{2,0,1:T(8,128)(2,1)}, u32[]{:S(2)}, u32[]{:S(2)}) async-start(bf16[128,8,128]{2,0,1:T(8,128)(2,1)} %copy_bitcast_fusion.3), calls=%async_computation.8 | async-start | bytes 524288 | tf_op jit(solution)/shard_map/all_to_all | solution.py:332
  174.6 11.8 %all-to-all-start.10 = ((bf16[128,8,128]{2,0,1:T(8,128)(2,1)}), bf16[128,8,128]{2,0,1:T(8,128)(2,1)}, u32[]{:S(2)}, u32[]{:S(2)}) async-start(bf16[128,8,128]{2,0,1:T(8,128)(2,1)} %copy_bitcast_fusion.2), calls=%async_computation.10 | async-start | bytes 524288 | tf_op jit(solution)/shard_map/all_to_all | solution.py:333
  186.4 31.5 %all-to-all-start.9 = ((bf16[128,8,512]{0,2,1:T(8,128)(2,1)}), bf16[128,8,512]{0,2,1:T(8,128)(2,1)S(1)}, u32[]{:S(2)}, u32[]{:S(2)}) async-start(bf16[128,8,512]{0,2,1:T(8,128)(2,1)} %bitcast.548), calls=%async_computation.9 | async-start | bytes 2097152 | tf_op jit(solution)/shard_map/all_to_all | solution.py:331
  197.4 26.8 %collective-permute-start = (bf16[1024,128]{1,0:T(8,128)(2,1)}, bf16[1024,128]{1,0:T(8,128)(2,1)}, u32[]{:S(2)}, u32[]{:S(2)}) collective-permute-start(bf16[1024,128]{1,0:T(8,128)(2,1)} %bitcast.102), channel_id=1, source_target_pairs={{0,24},{8,32},{16,40},{24,48},{32,56},{40,64},{48,72},{56,80},{64,... | collective-permute-start | bytes 786440 | tf_op jit(solution)/shard_map/ppermute | solution.py:43
  200.3 27.0 %collective-permute-start.1 = (bf16[1024,128]{1,0:T(8,128)(2,1)}, bf16[1024,128]{1,0:T(8,128)(2,1)}, u32[]{:S(2)}, u32[]{:S(2)}) collective-permute-start(bf16[1024,128]{1,0:T(8,128)(2,1)} %bitcast.102), channel_id=1, source_target_pairs={{0,16},{8,24},{16,32},{24,40},{32,48},{40,56},{48,64},{56,72},{64,... | collective-permute-start | bytes 786440 | tf_op jit(solution)/shard_map/ppermute | solution.py:43
  205.4 28.3 %collective-permute-start.2 = (bf16[1024,128]{1,0:T(8,128)(2,1)}, bf16[1024,128]{1,0:T(8,128)(2,1)}, u32[]{:S(2)}, u32[]{:S(2)}) collective-permute-start(bf16[1024,128]{1,0:T(8,128)(2,1)} %bitcast.102), channel_id=1, source_target_pairs={{0,8},{8,16},{16,24},{24,32},{32,40},{40,48},{48,56},{56,64},{64,7... | collective-permute-start | bytes 786440 | tf_op jit(solution)/shard_map/ppermute | solution.py:43
  207.4 41.8 %collective-permute-start.3 = (bf16[1024,128]{1,0:T(8,128)(2,1)}, bf16[1024,128]{1,0:T(8,128)(2,1)}, u32[]{:S(2)}, u32[]{:S(2)}) collective-permute-start(bf16[1024,128]{1,0:T(8,128)(2,1)} %bitcast.108), channel_id=1, source_target_pairs={{0,24},{8,32},{16,40},{24,48},{32,56},{40,64},{48,72},{56,80},{64,... | collective-permute-start | bytes 786440 | tf_op jit(solution)/shard_map/ppermute | solution.py:43
  212.4 44.4 %collective-permute-start.4 = (bf16[1024,128]{1,0:T(8,128)(2,1)}, bf16[1024,128]{1,0:T(8,128)(2,1)}, u32[]{:S(2)}, u32[]{:S(2)}) collective-permute-start(bf16[1024,128]{1,0:T(8,128)(2,1)} %bitcast.108), channel_id=1, source_target_pairs={{0,16},{8,24},{16,32},{24,40},{32,48},{40,56},{48,64},{56,72},{64,... | collective-permute-start | bytes 786440 | tf_op jit(solution)/shard_map/ppermute | solution.py:43
  217.9 55.6 %all-to-all-start.11 = ((bf16[128,8,512]{0,2,1:T(8,128)(2,1)}), bf16[128,8,512]{0,2,1:T(8,128)(2,1)}, u32[]{:S(2)}, u32[]{:S(2)}) async-start(bf16[128,8,512]{0,2,1:T(8,128)(2,1)} %bitcast.111), calls=%async_computation.11 | async-start | bytes 2097152 | tf_op jit(solution)/shard_map/all_to_all | solution.py:334
  224.1 304.3 %all-gather.9.cloned.1.call-start = ((), (), s32[]{:S(2)}) async-start(), calls=%async_computation.13 | async-start | bytes 2621440 | tf_op jit(solution)/shard_map/all_gather | solution.py:30
  224.1 43.3 %collective-permute-start.5 = (bf16[1024,128]{1,0:T(8,128)(2,1)}, bf16[1024,128]{1,0:T(8,128)(2,1)S(1)}, u32[]{:S(2)}, u32[]{:S(2)}) collective-permute-start(bf16[1024,128]{1,0:T(8,128)(2,1)} %bitcast.108), channel_id=1, source_target_pairs={{0,8},{8,16},{16,24},{24,32},{32,40},{40,48},{48,56},{56,64},{64,7... | collective-permute-start | bytes 786440 | tf_op jit(solution)/shard_map/ppermute | solution.py:43
  273.5 3.2 copy-start.30
  480.8 57.3 %all-to-all-start.12 = ((bf16[8,128,512]{2,1,0:T(8,128)(2,1)}), bf16[8,128,512]{2,1,0:T(8,128)(2,1)}, u32[]{:S(2)}, u32[]{:S(2)}) async-start(bf16[8,128,512]{2,1,0:T(8,128)(2,1)} %copy.289), calls=%async_computation.12 | async-start | bytes 2097152 | tf_op jit(solution)/shard_map/all_to_all | solution.py:357
  492.9 5.7 copy-start.31
  492.9 22.0 %copy-start.23 = (f32[4,16,256]{2,1,0:T(8,128)S(1)}, f32[4,16,256]{2,1,0:T(8,128)}, u32[]{:S(2)}) copy-start(f32[4,16,256]{2,1,0:T(8,128)} %reduce_window_sum.41) | copy-start | bytes 196612
  514.9 7.6 %copy-start.11 = (f32[1,1,16,64,128]{4,3,2,1,0:T(8,128)S(1)}, f32[1,1,16,64,128]{4,3,2,1,0:T(8,128)}, u32[]{:S(2)}) copy-start(f32[1,1,16,64,128]{4,3,2,1,0:T(8,128)} %get-tuple-element.672) | copy-start | bytes 1572868
  514.9 7.6 %copy-start.28 = (f32[16]{0:T(128)S(1)}, f32[16]{0:T(128)}, u32[]{:S(2)}) copy-start(f32[16]{0:T(128)} %copy-done.27) | copy-start | bytes 196
  514.9 7.6 %copy-start.29 = (f32[16]{0:T(128)S(1)}, f32[16]{0:T(128)}, u32[]{:S(2)}) copy-start(f32[16]{0:T(128)} %get-tuple-element.682) | copy-start | bytes 196
  522.5 4.0 copy-start.9
  522.5 4.0 copy-start.26
  526.6 1.9 copy-start.12
  528.4 4.0 copy-start.15
  528.4 5.0 copy-start.5
  528.4 5.0 copy-start.6
  535.3 11.5 %copy-start.14 = (bf16[128,8,128]{2,0,1:T(8,128)(2,1)S(1)}, bf16[128,8,128]{2,0,1:T(8,128)(2,1)}, u32[]{:S(2)}) copy-start(bf16[128,8,128]{2,0,1:T(8,128)(2,1)} %copy-done.13) | copy-start | bytes 786436
  538.1 19.9 %copy-start.10 = (bf16[4,256,16,64]{1,0,3,2:T(4,128)(2,1)S(1)}, bf16[4,256,16,64]{1,0,3,2:T(4,128)(2,1)}, u32[]{:S(2)}) copy-start(bf16[4,256,16,64]{1,0,3,2:T(4,128)(2,1)} %reshape.898) | copy-start | bytes 6291460
  538.1 19.9 %copy-start.20 = (pred[4,256,256]{2,1,0:T(8,128)(4,1)S(1)}, pred[4,256,256]{2,1,0:T(8,128)(4,1)}, u32[]{:S(2)}) copy-start(pred[4,256,256]{2,1,0:T(8,128)(4,1)} %compare_and_fusion.1) | copy-start | bytes 786436
  538.1 19.9 %copy-start.22 = (f32[4,256,1,16]{1,3,2,0:T(8,128)S(1)}, f32[4,256,1,16]{1,3,2,0:T(8,128)}, u32[]{:S(2)}) copy-start(f32[4,256,1,16]{1,3,2,0:T(8,128)} %copy-done.21) | copy-start | bytes 196612
  538.1 19.9 %copy-start.24 = (f32[4,16,256]{2,1,0:T(8,128)S(1)}, f32[4,16,256]{2,1,0:T(8,128)}, u32[]{:S(2)}) copy-start(f32[4,16,256]{2,1,0:T(8,128)} %reduce_window_sum.41) | copy-start | bytes 196612
  538.1 19.9 %copy-start.34 = (f32[16]{0:T(128)S(1)}, f32[16]{0:T(128)}, u32[]{:S(2)}) copy-start(f32[16]{0:T(128)} %dynamic_slice.121) | copy-start | bytes 196
  538.1 15.2 %all-to-all-start.7 = ((bf16[8,128,128]{2,1,0:T(8,128)(2,1)}), bf16[8,128,128]{2,1,0:T(8,128)(2,1)S(1)}, u32[]{:S(2)}, u32[]{:S(2)}) async-start(bf16[8,128,128]{2,1,0:T(8,128)(2,1)} %bitcast.99), calls=%async_computation.7 | async-start | bytes 524288 | tf_op jit(solution)/shard_map/all_to_all | solution.py:356
  553.3 21.9 %all-to-all-start.6 = ((bf16[8,128,128]{2,1,0:T(8,128)(2,1)}), bf16[8,128,128]{2,1,0:T(8,128)(2,1)S(1)}, u32[]{:S(2)}, u32[]{:S(2)}) async-start(bf16[8,128,128]{2,1,0:T(8,128)(2,1)} %bitcast.78), calls=%async_computation.6 | async-start | bytes 524288 | tf_op jit(solution)/shard_map/all_to_all | solution.py:355
  575.2 0.7 copy-start.17
  575.9 31.2 %all-to-all-start.5 = ((bf16[8,128,1024]{1,2,0:T(8,128)(2,1)}), bf16[8,128,1024]{1,2,0:T(8,128)(2,1)S(1)}, u32[]{:S(2)}, u32[]{:S(2)}) async-start(bf16[8,128,1024]{1,2,0:T(8,128)(2,1)} %copy.256), calls=%async_computation.5 | async-start | bytes 4194304 | tf_op jit(solution)/shard_map/all_to_all | solution.py:354
  607.1 2.9 copy-start.1
Sparse Core Ops, SparseCore 0:
  76.5 56.9 all-gather.14
  138.5 56.9 all-gather.12
  197.3 44.2 all-gather.10
  280.4 34.4 all-gather.8
where the time goes:
time: 628 us; the launch traced here: 617 us
  matrix products  196 us (31%)
  waiting for transfers between devices  118 us (19%)
  starting transfers between devices  94.8 us (15%)
  local copies, waits for them, and re-layouts  84.4 us (13%)
  other arithmetic  72.5 us (12%)
  blocking collectives  30.8 us (5%)
  between operations  14.9 us (2%)
    dot_general x8, matrix products, attend_block(): jnp.einsum('rqk,kd->qrd', grad_logits, key_block, preferred_element_type=...  60 us
    dot_general x8, matrix products, attend_block(): jnp.einsum('qrd,kd->rqk', grad_block, value_block, preferred_element_type...  55.8 us
    sub x8, matrix products, attend_block(): weights = jnp.exp(logits - row_peaks)  47.3 us
    ppermute x6, waiting for transfers between devices, from_behind(): lax.ppermute(value, axis, [(source, source + steps) for source in range(l...  37.8 us
    all_gather x3, blocking collectives, entering_2(): pieces = jax.tree.map(lambda part: lax.all_gather(part, axis), so_far)  30.8 us
    all_to_all x1, waiting for transfers between devices, shards(): lax.all_to_all(mixer_grad, 'head', split_axis=1, concat_axis=0, tiled=True)  25.5 us
    and x8, other arithmetic, attend_block(): (key_pos[None, :] <= query_pos[:, None]) & (key_pos[None, :] >= 0)  22.5 us
    all_to_all x1, waiting for transfers between devices, shards(): lax.all_to_all(mixer_input, 'head', split_axis=1, concat_axis=0, tiled=True)  22.2 us
  transfers between devices with their start and end apart: 23, of which 10 were waited for; matrix products, arithmetic and copies ran while one was open for 55% of the time, Pallas kernels for 0%

commit v1 on v0

v1 whole, which is shorter than its diff:
```python
import functools

import jax
import jax.numpy as jnp
from jax import lax
from jax.experimental import pallas as pl
from jax.experimental.pallas import tpu as pltpu
from jax.sharding import Mesh
from jax.sharding import PartitionSpec as P

MH = 128
HD = 64
NS = 128
DH = 128
BLOCK = 256
LOG2E = 1.4426950408889634
REACH = 3
QB = 128
KB = 256
NEG = -1e30

F32 = jnp.float32
BF16 = jnp.bfloat16


def dot_nt(a, b):
    return lax.dot_general(a, b, (((1,), (1,)), ((), ())), preferred_element_type=F32)


def dot_nn(a, b):
    return lax.dot_general(a, b, (((1,), (0,)), ((), ())), preferred_element_type=F32)


def dot_tn(a, b):
    return lax.dot_general(a, b, (((0,), (0,)), ((), ())), preferred_element_type=F32)


def attention_kernel(starts, first, qg, kv_all, out, kv, s_scr, gp_scr, m_scr, l_scr, c_scr, acc, sems):
    i = pl.program_id(0)
    rows = kv.shape[0] // (REACH + 1)
    lead = REACH * rows
    docs = starts.shape[0]

    @pl.when(i == 0)
    def _():
        c = pltpu.make_async_copy(kv_all, kv, sems.at[0])
        c.start()
        c.wait()

    base = first[0] - lead
    q0 = first[0] + i * QB
    qcol = lead + i * QB + lax.broadcasted_iota(jnp.int32, (QB, 1), 0)
    dcol = jnp.zeros((QB, 1), jnp.int32)
    low = jnp.int32(0)
    for j in range(docs):
        st = starts[j]
        low = jnp.where(st <= q0, st, low)
        dcol = jnp.where(st - base <= qcol, st - base, dcol)
    first_block = (low - base) // KB
    blocks = (lead + i * QB + QB - 1) // KB - first_block + 1
    heads = out.shape[1] // DH
    q = jnp.concatenate([qg[:, h * DH : (h + 1) * DH] for h in range(heads)], axis=0)
    g = jnp.concatenate([qg[:, (heads + h) * DH : (heads + h + 1) * DH] for h in range(heads)], axis=0)
    m_scr[...] = jnp.full(m_scr.shape, NEG, F32)
    l_scr[...] = jnp.zeros(l_scr.shape, F32)
    c_scr[...] = jnp.zeros(c_scr.shape, F32)
    acc[...] = jnp.zeros(acc.shape, F32)

    def scores(b, _):
        r0 = pl.multiple_of((first_block + b) * KB, KB)
        k = kv[pl.ds(r0, KB), 0:DH]
        v = kv[pl.ds(r0, KB), DH : 2 * DH]
        key = r0 + lax.broadcasted_iota(jnp.int32, (QB, KB), 1)
        ok = (key >= dcol) & (key <= qcol)
        s = dot_nt(q, k)
        gp_scr[b] = dot_nt(g, v)
        for h in range(heads):
            sh = jnp.where(ok, s[h * QB : (h + 1) * QB], NEG)
            s_scr[b, h * QB : (h + 1) * QB, :] = sh
            top = m_scr[h * QB : (h + 1) * QB, :]
            for n in range(KB // 128):
                top = jnp.maximum(top, sh[:, n * 128 : (n + 1) * 128])
            m_scr[h * QB : (h + 1) * QB, :] = top
        return 0

    lax.fori_loop(0, blocks, scores, 0)
    scale = DH**-0.5 * LOG2E
    peak = jnp.max(m_scr[...], axis=1, keepdims=True)

    def weights(b, _):
        e = jnp.exp2((s_scr[b] - peak) * scale)
        s_scr[b] = e
        eg = e * gp_scr[b]
        l = l_scr[...]
        c = c_scr[...]
        for n in range(KB // 128):
            l += e[:, n * 128 : (n + 1) * 128]
            c += eg[:, n * 128 : (n + 1) * 128]
        l_scr[...] = l
        c_scr[...] = c
        return 0

    lax.fori_loop(0, blocks, weights, 0)
    total = jnp.sum(l_scr[...], axis=1, keepdims=True)
    centre = jnp.sum(c_scr[...], axis=1, keepdims=True) / total

    def grads(b, _):
        r0 = pl.multiple_of((first_block + b) * KB, KB)
        k = kv[pl.ds(r0, KB), 0:DH]
        ds = (s_scr[b] * (gp_scr[b] - centre)).astype(BF16)
        acc[...] += dot_nn(ds, k)
        return 0

    lax.fori_loop(0, blocks, grads, 0)
    res = (acc[...] * (DH**-0.5 / total)).astype(BF16)
    for h in range(heads):
        out[:, h * DH : (h + 1) * DH] = res[h * QB : (h + 1) * QB]


def attention(qg, kv, starts, first):
    rows = qg.shape[0]
    heads = qg.shape[1] // (2 * DH)
    lead = REACH * rows
    most = (lead + QB) // KB + 2
    hq = heads * QB
    return pl.pallas_call(
        attention_kernel,
        grid_spec=pltpu.PrefetchScalarGridSpec(
            num_scalar_prefetch=2,
            grid=(rows // QB,),
            in_specs=[pl.BlockSpec((QB, qg.shape[1]), lambda i, *_: (i, 0))]
            + [pl.BlockSpec(memory_space=pltpu.HBM)],
            out_specs=pl.BlockSpec((QB, heads * DH), lambda i, *_: (i, 0)),
            scratch_shapes=[
                pltpu.VMEM((lead + rows, 2 * DH), BF16),
                pltpu.VMEM((most, hq, KB), F32),
                pltpu.VMEM((most, hq, KB), F32),
                pltpu.VMEM((hq, 128), F32),
                pltpu.VMEM((hq, 128), F32),
                pltpu.VMEM((hq, 128), F32),
                pltpu.VMEM((hq, DH), F32),
                pltpu.SemaphoreType.DMA((1,)),
            ],
        ),
        out_shape=jax.ShapeDtypeStruct((rows, heads * DH), BF16),
        compiler_params=pltpu.CompilerParams(vmem_limit_bytes=56 << 20),
        cost_estimate=pl.CostEstimate(flops=12 * 10**9, bytes_accessed=6 << 20, transcendentals=16 * 10**6),
        name="attention",
    )(starts, first, qg, kv)


def split_sum(tri, dl):
    a = dl.astype(BF16)
    rest = dl - a.astype(F32)
    b = rest.astype(BF16)
    c = (rest - b.astype(F32)).astype(BF16)
    return dot_nn(tri, a) + dot_nn(tri, b) + dot_nn(tri, c)


def iota(shape, dim):
    return lax.broadcasted_iota(jnp.int32, shape, dim)


def doc_of(starts, pos):
    d = jnp.zeros(pos.shape, jnp.int32)
    for j in range(starts.shape[0]):
        d += (starts[j] <= pos).astype(jnp.int32)
    return d


def widen(values, spread):
    hi = values.astype(BF16)
    lo = (values - hi.astype(F32)).astype(BF16)
    return dot_nn(hi, spread) + dot_nn(lo, spread)


def edges(starts, first, c, st, rates):
    tri = (iota((BLOCK, BLOCK), 0) >= iota((BLOCK, BLOCK), 1)).astype(BF16)
    cum = split_sum(tri, st.astype(F32) * rates)
    begin = first + c * BLOCK
    doc_col = doc_of(starts, begin + iota((BLOCK, 1), 0))
    doc_last = doc_of(starts, begin + BLOCK - 1 + iota((1, 1), 0))
    doc_prev = doc_of(starts, begin - 1 + iota((1, 1), 0))
    total = cum[BLOCK - 1 : BLOCK, :]
    entering = jnp.exp2(jnp.where(doc_col == doc_prev, cum, NEG))
    to_end = jnp.exp2(jnp.where(doc_col == doc_last, total - cum, NEG))
    return cum, entering, to_end, doc_last == doc_prev


def spread_matrix(columns, group):
    return (iota((128, columns), 0) == group * (columns // HD) + iota((128, columns), 1) // HD).astype(BF16)


def edge_scratch(starts, first, st, rates, cum, cum_t, entering, to_end):
    @pl.when(pl.program_id(0) == 0)
    def _():
        a, b, c, _ = edges(starts, first[0], 0, st[...], rates[...])
        cum[...] = a
        cum_t[...] = jnp.transpose(a)
        entering[...] = b
        to_end[...] = c


MESH = pl.DeviceIdType.MESH


def links_of(rows):
    n = rows.shape[0] // 2
    return rows[0:n, :].astype(F32) + rows[n : 2 * n, :].astype(F32)


def first_kernel(
    starts, x, g, w, r, st, q, k, v, ag, rates,
    xs_out, gs_out, ws_out, rs_out, st_out, kv, qg, both,
    xs, gs, ws, rs, sts, ends_send, ends, lk, state, back, fs, fr, bs, br,
    own_sem, pair_send, pair_recv, head_send, head_recv, ends_ssem, ends_rsem, ring_ssem, ring_rsem, out_sem,
):
    ctx, hx, core = lax.axis_index("ctx"), lax.axis_index("hx"), lax.axis_index("core")
    slabs, chips, cores = lax.axis_size("ctx"), lax.axis_size("hx"), lax.axis_size("core")
    parts = chips * cores
    me = hx * cores + core
    other = 1 - core
    tokens = x.shape[0]
    rows = tokens * parts
    half = x.shape[1] // cores
    thin = w.shape[1] // cores
    qw = q.shape[1] // parts
    columns = half // chips
    heads = columns // HD
    begin = ctx * rows + hx * BLOCK

    def peer(d):
        p = lax.rem(me + d, parts)
        return p, {"hx": p // cores, "core": lax.rem(p, cores)}

    after = {"ctx": lax.rem(ctx + 1, slabs)}
    ahead = {"ctx": lax.rem(ctx + slabs - 1, slabs)}

    barrier = pltpu.get_barrier_semaphore()
    for d in range(1, parts):
        pl.semaphore_signal(barrier, inc=1, device_id=peer(d)[1], device_id_type=MESH)
    for n in (after, ahead):
        pl.semaphore_signal(barrier, inc=1, device_id=n, device_id_type=MESH)
    pl.semaphore_wait(barrier, parts + 1)

    def remote(src, dst, ssem, rsem, device):
        return pltpu.make_async_remote_copy(
            src_ref=src, dst_ref=dst, send_sem=ssem, recv_sem=rsem, device_id=device, device_id_type=MESH
        )

    def cols(n, width):
        return pl.ds(pl.multiple_of(n * width, 128), width)

    mine = pl.ds(pl.multiple_of(core * tokens, 128), tokens)
    pairs, owns = [], []
    for n, (src, dst, width) in enumerate(((x, xs, half), (g, gs, half), (w, ws, thin), (r, rs, thin), (st, sts, None))):
        theirs = src if width is None else src.at[:, cols(other, width)]
        ours = src if width is None else src.at[:, cols(core, width)]
        pairs.append(remote(theirs, dst.at[mine, :], pair_send.at[n], pair_recv.at[n], {"core": other}))
        owns.append(pltpu.make_async_copy(ours, dst.at[mine, :], own_sem.at[n]))
    for c in pairs + owns:
        c.start()
    lead = REACH * rows
    mine_kv = pl.ds(pl.multiple_of(lead + me * tokens, 128), tokens)
    mine_q = pl.ds(pl.multiple_of(me * tokens, 128), tokens)
    kv_moves, qg_moves, kv_own, qg_own = [], [], [], []
    for n, (src, dst, width, at, into, own) in enumerate(
        (
            (k, kv, DH, mine_kv, kv_moves, kv_own),
            (v, kv, DH, mine_kv, kv_moves, kv_own),
            (q, qg, qw, mine_q, qg_moves, qg_own),
            (ag, qg, qw, mine_q, qg_moves, qg_own),
        )
    ):
        place = slice((n % 2) * width, (n % 2 + 1) * width)
        for d in range(1, parts):
            p, device = peer(d)
            into.append(
                remote(src.at[:, cols(p, width)], dst.at[at, place], head_send.at[n, d], head_recv.at[n, d], device)
            )
        own.append(pltpu.make_async_copy(src.at[:, cols(me, width)], dst.at[at, place], own_sem.at[5 + n]))
    for c in kv_moves + kv_own + qg_own:
        c.start()

    for c in owns:
        c.wait()
    for c in pairs:
        c.wait_recv()
    outs = [
        pltpu.make_async_copy(src, dst, out_sem.at[n])
        for n, (src, dst) in enumerate(((xs, xs_out), (gs, gs_out), (ws, ws_out), (rs, rs_out), (sts, st_out)))
    ]
    for c in outs:
        c.start()

    cum, entering, to_end, linked = edges(starts, begin, 0, sts[...], rates[...])
    entering_hi = entering.astype(BF16)
    entering_lo = (entering - entering_hi.astype(F32)).astype(BF16)
    to_end_hi = to_end.astype(BF16)
    to_end_lo = (to_end - to_end_hi.astype(F32)).astype(BF16)
    tot = jnp.transpose(jnp.broadcast_to(cum[BLOCK - 1 : BLOCK, :], (128, 128)))
    link_all = jnp.exp2(jnp.where(linked, tot, NEG))

    def make_ends(group, out):
        spread = spread_matrix(columns, core * chips + group)
        wide_end = dot_nn(to_end_hi, spread) + dot_nn(to_end_lo, spread)
        wide_enter = dot_nn(entering_hi, spread) + dot_nn(entering_lo, spread)
        iw = (xs[:, cols(group, columns)].astype(F32) * wide_end).astype(BF16)
        gw = (gs[:, cols(group, columns)].astype(F32) * wide_enter).astype(BF16)
        out[0:columns, :] = dot_tn(iw, ws[:, cols(group, NS)]).astype(BF16)
        out[columns : 2 * columns, :] = dot_tn(gw, rs[:, cols(group, NS)]).astype(BF16)
        pick = (iota((heads, 128), 1) == (core * chips + group) * heads + iota((heads, 128), 0)).astype(F32)
        link = lax.dot_general(
            pick, link_all, (((1,), (0,)), ((), ())), precision=lax.Precision.HIGHEST, preferred_element_type=F32
        )
        hi = link.astype(BF16)
        out[2 * columns : 2 * columns + heads, :] = hi
        out[2 * columns + heads : 2 * columns + 2 * heads, :] = (link - hi.astype(F32)).astype(BF16)

    end_moves = []
    for d in range(1, chips):
        to = lax.rem(hx + d, chips)
        make_ends(to, ends_send.at[d - 1])
        c = remote(ends_send.at[d - 1], ends.at[hx], ends_ssem.at[d], ends_rsem.at[d], {"hx": to})
        c.start()
        end_moves.append(c)
    for c in qg_moves:
        c.start()
    make_ends(hx, ends.at[hx])

    for c in kv_own:
        c.wait()
    for c in kv_moves:
        c.wait_recv()
    hops = []
    for n in range(REACH):
        src = pl.ds((REACH - n) * rows, rows)
        dst = pl.ds((REACH - n - 1) * rows, rows)
        hops.append(remote(kv.at[src, :], kv.at[dst, :], ring_ssem.at[n], ring_rsem.at[n], after))
    for n in range(REACH):
        if n > 0:
            hops[n - 1].wait_recv()
        hops[n].start()

    for c in end_moves:
        c.wait_recv()
    for n in range(chips):
        lk[n] = links_of(ends[n, 2 * columns :, :])
    prods = [None, lk[0]]
    for n in range(1, chips):
        prods.append(prods[-1] * lk[n])
    for n in range(1, chips + 1):
        lk[chips + n - 1] = prods[n]
    whole = 2 * chips - 1

    def head_rows(h):
        return pl.ds(pl.multiple_of(h * HD, HD), HD), pl.ds(pl.multiple_of(columns + h * HD, HD), HD)

    def totals(h, _):
        at, bt = head_rows(h)
        one = pl.ds(h, 1)
        s = ends[0, at, :].astype(F32)
        b = ends[0, bt, :].astype(F32)
        for n in range(1, chips):
            s = lk[n, one, :] * s + ends[n, at, :].astype(F32)
            b = b + lk[chips + n - 1, one, :] * ends[n, bt, :].astype(F32)
        state[at, :] = s
        back[at, :] = b
        fs[0, at, :] = s.astype(BF16)
        bs[0, at, :] = b.astype(BF16)
        return 0

    lax.fori_loop(0, heads, totals, 0)
    fwd = [remote(fs.at[n], fr.at[n], ring_ssem.at[3 + n], ring_rsem.at[3 + n], after) for n in range(REACH)]
    bwd = [remote(bs.at[n], br.at[n], ring_ssem.at[6 + n], ring_rsem.at[6 + n], ahead) for n in range(REACH)]
    fwd[0].start()
    bwd[0].start()
    for n in range(1, REACH):
        for moves, base, recv, send in ((bwd, back, br, bs), (fwd, state, fr, fs)):
            moves[n - 1].wait_recv()

            def step(h, _):
                at, unused = head_rows(h)
                val = base[at, :] + lk[whole, pl.ds(h, 1), :] * recv[n - 1, at, :].astype(F32)
                send[n, at, :] = val.astype(BF16)
                return 0

            lax.fori_loop(0, heads, step, 0)
            moves[n].start()
    fwd[REACH - 1].wait_recv()
    bwd[REACH - 1].wait_recv()

    def chip_states(h, _):
        at, bt = head_rows(h)
        one = pl.ds(h, 1)
        s = fr[REACH - 1, at, :].astype(F32)
        b = br[REACH - 1, at, :].astype(F32)
        for n in range(chips):
            both[n, at, :] = s.astype(BF16)
            s = lk[n, one, :] * s + ends[n, at, :].astype(F32)
        for n in reversed(range(chips)):
            both[n, bt, :] = b.astype(BF16)
            b = lk[n, one, :] * b + ends[n, bt, :].astype(F32)
        return 0

    lax.fori_loop(0, heads, chip_states, 0)
    hops[REACH - 1].wait_recv()
    for c in qg_own + outs:
        c.wait()
    for c in qg_moves:
        c.wait_recv()
    for c in pairs + kv_moves + qg_moves + end_moves + hops + fwd + bwd:
        c.wait_send()


def first_stage(starts, x, g, w, r, st, q, k, v, ag, rates, parts, cores):
    chips = parts // cores
    tokens = x.shape[0]
    rows = tokens * parts
    half, thin = x.shape[1] // cores, w.shape[1] // cores
    columns = half // chips
    heads = columns // HD
    packed = 2 * columns + 2 * heads
    both_rows = cores * tokens
    hbm = pl.BlockSpec(memory_space=pltpu.HBM)
    vmem = pl.BlockSpec(memory_space=pltpu.VMEM)
    dma = pltpu.SemaphoreType.DMA
    return pl.pallas_call(
        first_kernel,
        in_specs=[pl.BlockSpec(memory_space=pltpu.SMEM)] + [hbm] * 9 + [vmem],
        out_specs=[hbm] * 7 + [vmem],
        out_shape=[
            jax.ShapeDtypeStruct((both_rows, half), BF16),
            jax.ShapeDtypeStruct((both_rows, half), BF16),
            jax.ShapeDtypeStruct((both_rows, thin), BF16),
            jax.ShapeDtypeStruct((both_rows, thin), BF16),
            jax.ShapeDtypeStruct((both_rows, st.shape[1]), BF16),
            jax.ShapeDtypeStruct(((REACH + 1) * rows, 2 * DH), BF16),
            jax.ShapeDtypeStruct((rows, 2 * q.shape[1] // parts), BF16),
            jax.ShapeDtypeStruct((chips, 2 * columns, NS), BF16),
        ],
        scratch_shapes=[
            pltpu.VMEM((both_rows, half), BF16),
            pltpu.VMEM((both_rows, half), BF16),
            pltpu.VMEM((both_rows, thin), BF16),
            pltpu.VMEM((both_rows, thin), BF16),
            pltpu.VMEM((both_rows, st.shape[1]), BF16),
            pltpu.VMEM((chips - 1, packed, NS), BF16),
            pltpu.VMEM((chips, packed, NS), BF16),
            pltpu.VMEM((2 * chips, heads, 128), F32),
            pltpu.VMEM((columns, NS), F32),
            pltpu.VMEM((columns, NS), F32),
            pltpu.VMEM((REACH, columns, NS), BF16),
            pltpu.VMEM((REACH, columns, NS), BF16),
            pltpu.VMEM((REACH, columns, NS), BF16),
            pltpu.VMEM((REACH, columns, NS), BF16),
            dma((9,)),
            dma((5,)),
            dma((5,)),
            dma((4, parts)),
            dma((4, parts)),
            dma((chips,)),
            dma((chips,)),
            dma((9,)),
            dma((9,)),
            dma((5,)),
        ],
        compiler_params=pltpu.CompilerParams(vmem_limit_bytes=60 << 20, collective_id=0, has_side_effects=True),
        cost_estimate=pl.CostEstimate(flops=2 * 10**9, bytes_accessed=16 << 20, transcendentals=10**5),
        name="first_stage",
    )(starts, x, g, w, r, st, q, k, v, ag, rates)


EDGES = [
    pltpu.VMEM((BLOCK, 128), F32),
    pltpu.VMEM((128, BLOCK), F32),
    pltpu.VMEM((BLOCK, 128), F32),
    pltpu.VMEM((BLOCK, 128), F32),
]


def grads_kernel(starts, first, core, x, g, w, r, st, rates, skips, both, out_x, out_w, out_r, cum, cum_t, entering, to_end):
    j = pl.program_id(0)
    columns = x.shape[1]
    heads = columns // HD
    edge_scratch(starts, first, st, rates, cum, cum_t, entering, to_end)
    begin = first[0]
    doc_col = doc_of(starts, begin + iota((BLOCK, 1), 0))
    doc_row = doc_of(starts, begin + iota((1, BLOCK), 1))
    ok = (iota((BLOCK, BLOCK), 0) <= iota((BLOCK, BLOCK), 1)) & (doc_col == doc_row)
    group = core[0] * pl.num_programs(0) + j
    spread = spread_matrix(columns, group)
    end_wide = widen(to_end[...], spread)
    iw = (x[...].astype(F32) * end_wide).astype(BF16)
    gw = (g[...].astype(F32) * widen(entering[...], spread)).astype(BF16)
    wv = w[...]
    rv = r[...]
    state = both[0, 0:columns, :]
    back = both[0, columns : 2 * columns, :]
    carried = dot_nt(wv, back)
    scores = dot_nt(wv, rv)
    joint = jnp.zeros((BLOCK, BLOCK), F32)
    lane = iota((BLOCK, 2 * HD), 1) < HD
    offset = pl.multiple_of(group * heads, heads)
    rows_t = cum_t[pl.ds(offset, heads), :]
    cols_all = jnp.transpose(jnp.concatenate([rows_t, jnp.zeros((128 - heads, BLOCK), F32)], axis=0))
    for p in range(heads // 2):
        cols = slice(p * 2 * HD, (p + 1) * 2 * HD)
        xp = x[:, cols]
        gp = g[:, cols]
        zero = jnp.zeros_like(xp)
        inner = skips[:, cols] * gp.astype(F32) + end_wide[:, cols] * carried[:, cols]
        for half in range(2):
            h = 2 * p + half
            mine = lane if half == 0 else ~lane
            decay = jnp.exp2(jnp.where(ok, rows_t[h : h + 1, :] - cols_all[:, h : h + 1], NEG))
            joint += decay * dot_nt(jnp.where(mine, xp, zero), gp)
            mixing = (scores * decay).astype(BF16)
            inner += dot_nn(mixing, jnp.where(mine, gp, zero))
        out_x[:, cols] = inner.astype(BF16)
    low = joint.astype(BF16)
    out_w[...] = (dot_nn(low, rv) + dot_nn(iw, back)).astype(BF16)
    out_r[...] = (dot_tn(low, wv) + dot_nn(gw, state)).astype(BF16)


def mixer_grads(mix, rates, skips, both, starts, first, core, columns, groups):
    return pl.pallas_call(
        grads_kernel,
        grid_spec=pltpu.PrefetchScalarGridSpec(
            num_scalar_prefetch=3,
            grid=(groups,),
            in_specs=[
                pl.BlockSpec((BLOCK, columns), lambda j, *_: (0, j)),
                pl.BlockSpec((BLOCK, columns), lambda j, *_: (0, j)),
                pl.BlockSpec((BLOCK, NS), lambda j, *_: (0, j)),
                pl.BlockSpec((BLOCK, NS), lambda j, *_: (0, j)),
                pl.BlockSpec((BLOCK, 128), lambda j, *_: (0, 0)),
                pl.BlockSpec((1, 128), lambda j, *_: (0, 0)),
                pl.BlockSpec((1, columns), lambda j, *_: (0, j)),
                pl.BlockSpec((1, 2 * columns, NS), lambda j, *_: (j, 0, 0)),
            ],
            out_specs=[
                pl.BlockSpec((BLOCK, columns), lambda j, *_: (0, j)),
                pl.BlockSpec((BLOCK, NS), lambda j, *_: (0, j)),
                pl.BlockSpec((BLOCK, NS), lambda j, *_: (0, j)),
            ],
            scratch_shapes=EDGES,
        ),
        out_shape=[
            jax.ShapeDtypeStruct((BLOCK, groups * columns), BF16),
            jax.ShapeDtypeStruct((BLOCK, groups * NS), BF16),
            jax.ShapeDtypeStruct((BLOCK, groups * NS), BF16),
        ],
        compiler_params=pltpu.CompilerParams(vmem_limit_bytes=40 << 20),
        cost_estimate=pl.CostEstimate(flops=8 * 10**9, bytes_accessed=14 << 20, transcendentals=5 * 10**6),
        name="mixer_grads",
    )(starts, first, core, *mix, rates, skips, both)


def unpack(moved):
    return moved.transpose(1, 0, 2).reshape(moved.shape[1], -1)


HEAD = ("hx", "core")


def shards(x, w, r, steps, fast_rates, slow_heads, skip_gains, grad, q, k, v, ag, doc_lengths):
    parts = lax.axis_size(HEAD)
    chips = lax.axis_size("hx")
    cores = lax.axis_size("core")
    tokens = x.shape[0]
    rows = tokens * parts
    columns = x.shape[1] // parts
    local_heads = MH // cores
    total_rows = rows * lax.axis_size("ctx")
    slab = (lax.axis_index("ctx") * rows).astype(jnp.int32)
    starts = (jnp.cumsum(doc_lengths) - doc_lengths).astype(jnp.int32)
    slab_first = slab.reshape(1)
    chip_first = (slab + lax.axis_index("hx") * BLOCK).astype(jnp.int32).reshape(1)

    slow = jnp.any(jnp.arange(MH, dtype=jnp.int32)[:, None] == slow_heads[None, :], axis=1)
    rates = jnp.where(slow, 1.0 / total_rows, fast_rates) * -LOG2E
    rates = rates.reshape(1, MH)
    core = lax.axis_index("core").astype(jnp.int32).reshape(1)
    skips = lax.dynamic_slice_in_dim(skip_gains, lax.axis_index("core") * local_heads, local_heads)
    skips = jnp.repeat(skips, HD).reshape(1, local_heads * HD)

    *mix, kv, qg, both = first_stage(starts, x, grad, w, r, steps, q, k, v, ag, rates, parts, cores)
    both = lax.all_to_all(both, "hx", split_axis=0, concat_axis=0, tiled=True)
    grad_q = attention(qg, kv, starts, slab_first)
    grad_q, both = lax.optimization_barrier((grad_q, both))
    moved = lax.all_to_all(grad_q, HEAD, split_axis=0, concat_axis=0, tiled=True)
    grad_q = unpack(moved.reshape(parts, tokens, -1))

    gx, gw, gr = mixer_grads(mix, rates, skips, both, starts, chip_first, core, columns, chips)
    joined = jnp.concatenate([gx, gw, gr], axis=1)
    moved = lax.all_to_all(joined, "core", split_axis=0, concat_axis=0, tiled=True)
    moved = moved.reshape(cores, tokens, -1)
    wide = local_heads * HD
    thin = chips * NS
    return (
        unpack(moved[:, :, :wide]),
        unpack(moved[:, :, wide : wide + thin]),
        unpack(moved[:, :, wide + thin :]),
        grad_q,
    )


def solution(mesh):
    split = Mesh(mesh.devices.reshape(mesh.shape["ctx"], -1, 2), ("ctx", "hx", "core"))
    tokens = P(("ctx", "hx", "core"), None)
    return jax.shard_map(
        shards,
        mesh=split,
        in_specs=(tokens, tokens, tokens, tokens, P(), P(), P(), tokens, tokens, tokens, tokens, tokens, P()),
        out_specs=(tokens, tokens, tokens, tokens),
        check_vma=False,
    )
```

time: 628 us -> 198 us (0.32)
  the two profiles are of different devices: /device:TPU:1 before, /device:TPU:128 now
where the time goes in v1:
time: 198 us
  Pallas kernels  157 us (79%)
  waiting for transfers between devices  13 us (7%)
  local copies, waits for them, and re-layouts  9.57 us (5%)
  starting transfers between devices  8.53 us (4%)
  blocking collectives  5.84 us (3%)
  other arithmetic  3.46 us (2%)
    pallas_call x1, Pallas kernels, first_stage(): pl.pallas_call(first_kernel, in_specs=[pl.BlockSpec(memory_space=pltpu.SM...  76.3 us
    pallas_call x1, Pallas kernels, attention(): pl.pallas_call(attention_kernel, grid_spec=pltpu.PrefetchScalarGridSpec(n...  66.7 us
    pallas_call x1, Pallas kernels, mixer_grads(): pl.pallas_call(grads_kernel, grid_spec=pltpu.PrefetchScalarGridSpec(num_s...  13.7 us
    all_to_all x1, waiting for transfers between devices, shards(): lax.all_to_all(grad_q, HEAD, split_axis=0, concat_axis=0, tiled=True)  13 us
    all_to_all x1, blocking collectives, shards(): lax.all_to_all(joined, 'core', split_axis=0, concat_axis=0, tiled=True)  5.84 us
    reshape x4, local copies, waits for them, and re-layouts, unpack(): return moved.transpose(1, 0, 2).reshape(moved.shape[1], -1)  5.22 us
    all_to_all x1, starting transfers between devices, shards(): lax.all_to_all(grad_q, HEAD, split_axis=0, concat_axis=0, tiled=True)  4.81 us
  transfers between devices with their start and end apart: 2, of which 1 were waited for; matrix products, arithmetic and copies ran while one was open for 2% of the time, Pallas kernels for 34%

profile of v1, /device:TPU:128, one launch (start us, length us, event | category | flops | bytes accessed | tf_op | source)
XLA Modules:
  0.0 197.9 jit_solution(425490280906537024)
XLA Ops:
  0.6 0.7 copy.27
  1.4 0.1 reduce
  1.5 1.2 sub.3.starts
  2.7 0.7 fusion
  3.4 1.2 multiply_bitcast_fusion.rates
  4.6 76.3 %first_stage.1 = (bf16[256,4096]{1,0:T(8,128)(2,1)}, bf16[256,4096]{1,0:T(8,128)(2,1)}, bf16[256,512]{1,0:T(8,128)(2,1)}, bf16[256,512]{1,0:T(8,128)(2,1)}, bf16...) custom-call(s32[16]{0:T(128)} %sub.3.starts, ...), custom_call_target="tpu_custom_call" | custom-call | flops 2000000000 | bytes 16777216 | tf_op jit(solution)/shard_map/first_stage/pallas_call | solution.py:428
  81.0 0.0 copy-start.7
  81.0 3.7 %all-to-all-start = ((bf16[4,2048,128]{2,1,0:T(8,128)(2,1)}), bf16[4,2048,128]{2,1,0:T(8,128)(2,1)S(1)}, u32[]{:S(2)}, u32[]{:S(2)}) async-start(bf16[4,2048,128]{2,1,0:T(8,128)(2,1)} %get-tuple-element.24), calls=%async_computation | async-start | bytes 4194304 | tf_op jit(solution)/shard_map/all_to_all | solution.py:589
  84.7 0.0 copy-done.7
  84.7 0.1 dynamic_slice.3
  84.8 0.1 broadcast_in_dim.10
  84.9 0.1 reshape_reshape.3.skips
  85.0 0.0 copy-start
  85.0 0.0 copy-start.1
  85.0 0.0 copy-start.4
  85.0 0.0 copy-start.5
  85.0 0.0 copy-start.6
  85.0 66.7 %attention.1 = bf16[1024,512]{1,0:T(8,128)(2,1)} custom-call(s32[16]{0:T(128)} %sub.3.starts, s32[1]{0:T(128)} %bitcast.4.first, bf16[1024,1024]{1,0:T(8,128)(2,1)} %get-tuple-element.22.qg, bf16[4096,256]{1,0:T(8,128)(2,1)} %get-tuple-element.23.kv_all), custom_call_target="tpu_custom_call" | custom-call | flops 12000000000 | bytes 6291456 | tf_op jit(solution)/shard_map/attention/pallas_call | solution.py:126
  151.7 0.0 all-to-all-done.both
  151.7 0.0 copy-done
  151.7 0.0 copy-done.1
  151.7 0.0 copy-done.4
  151.7 0.0 copy-done.5
  151.7 0.0 copy-done.6
  151.7 0.0 copy-start.2
  151.7 1.6 copy-done.2
  153.3 0.0 copy-start.3
  153.3 1.6 copy-done.3
  154.9 13.7 %mixer_grads.1 = (bf16[256,4096]{1,0:T(8,128)(2,1)S(1)}, bf16[256,512]{1,0:T(8,128)(2,1)S(1)}, bf16[256,512]{1,0:T(8,128)(2,1)S(1)}) custom-call(s32[16]{0:T(128)S(1)} %copy-done, s32[1]{0:T(128)} %bitcast.1.first, s32[1]{0:T(128)} %bitcast.2.core, bf16[256,4096]{1,0:T(8,128)(2,1)S(1)} %copy-done.2, bf16[256,4096]{1,0:T(8,128)(2,1)S(1)} %copy-done.3, ...), custom_call_target="tpu_custom_call" | custom-call | flops 8000000000 | bytes 14680064 | tf_op jit(solution)/shard_map/mixer_grads/pallas_call | solution.py:527
  168.7 0.2 pad_maximum_fusion
  168.9 5.8 %all_to_all.23 = bf16[2,128,5120]{2,1,0:T(8,128)(2,1)S(1)} all-to-all(bf16[2,128,5120]{2,1,0:T(8,128)(2,1)S(1)} %bitcast.23), channel_id=1, replica_groups=mesh['ctx'=32,'hx'=4,'core'=2] {'core'}, dimensions={0} | all-to-all | bytes 5242880 | tf_op jit(solution)/shard_map/all_to_all | solution.py:597
  174.7 4.8 %all-to-all-start.2 = ((bf16[8,128,512]{2,1,0:T(8,128)(2,1)}), bf16[8,128,512]{2,1,0:T(8,128)(2,1)}, u32[]{:S(2)}, u32[]{:S(2)}) async-start(bf16[8,128,512]{2,1,0:T(8,128)(2,1)} %bitcast.25), calls=%async_computation.2 | async-start | bytes 2097152 | tf_op jit(solution)/shard_map/all_to_all | solution.py:592
  179.5 0.1 slice_bitcast_fusion
  179.7 1.5 copy.32
  181.1 0.7 copy.33
  181.9 0.7 copy.34
  182.6 13.0 %all-to-all-done.2 = bf16[8,128,512]{2,1,0:T(8,128)(2,1)} async-done(((bf16[8,128,512]{2,1,0:T(8,128)(2,1)}), bf16[8,128,512]{2,1,0:T(8,128)(2,1)}, u32[]{:S(2)}, u32[]{:S(2)}) %all-to-all-start.2) | async-done | bytes 1048608 | tf_op jit(solution)/shard_map/all_to_all | solution.py:592
  195.6 2.3 %copy.35 = bf16[8,16,8,512]{3,2,0,1:T(8,128)(2,1)} copy(bf16[8,16,8,512]{3,2,1,0:T(8,128)(2,1)} %bitcast.17) | data formatting | bytes 2097152 | tf_op jit(solution)/shard_map/reshape | solution.py:561
  (2 shorter events, 0.1 us)
Async XLA Ops:
  81.0 3.7 %copy-start.7 = (f32[128]{0:T(128)S(1)}, f32[128]{0:T(128)}, u32[]{:S(2)}) copy-start(f32[128]{0:T(128)} %param.19) | copy-start | bytes 1540
  81.0 70.7 %all-to-all-start = ((bf16[4,2048,128]{2,1,0:T(8,128)(2,1)}), bf16[4,2048,128]{2,1,0:T(8,128)(2,1)S(1)}, u32[]{:S(2)}, u32[]{:S(2)}) async-start(bf16[4,2048,128]{2,1,0:T(8,128)(2,1)} %get-tuple-element.24), calls=%async_computation | async-start | bytes 4194304 | tf_op jit(solution)/shard_map/all_to_all | solution.py:589
  85.0 66.7 %copy-start = (s32[16]{0:T(128)S(1)}, s32[16]{0:T(128)}, u32[]{:S(2)}) copy-start(s32[16]{0:T(128)} %sub.3.starts) | copy-start | bytes 196
  85.0 66.7 %copy-start.1 = (f32[1,128]{1,0:T(1,128)S(1)}, f32[1,128]{1,0:T(1,128)}, u32[]{:S(2)}) copy-start(f32[1,128]{1,0:T(1,128)} %multiply_bitcast_fusion.rates) | copy-start | bytes 1540
  85.0 66.7 %copy-start.4 = (bf16[256,512]{1,0:T(8,128)(2,1)S(1)}, bf16[256,512]{1,0:T(8,128)(2,1)}, u32[]{:S(2)}) copy-start(bf16[256,512]{1,0:T(8,128)(2,1)} %get-tuple-element.19.w) | copy-start | bytes 786436
  85.0 66.7 %copy-start.5 = (bf16[256,512]{1,0:T(8,128)(2,1)S(1)}, bf16[256,512]{1,0:T(8,128)(2,1)}, u32[]{:S(2)}) copy-start(bf16[256,512]{1,0:T(8,128)(2,1)} %get-tuple-element.20.r) | copy-start | bytes 786436
  85.0 66.7 %copy-start.6 = (bf16[256,128]{1,0:T(8,128)(2,1)S(1)}, bf16[256,128]{1,0:T(8,128)(2,1)}, u32[]{:S(2)}) copy-start(bf16[256,128]{1,0:T(8,128)(2,1)} %get-tuple-element.21.st) | copy-start | bytes 196612
  151.7 1.6 copy-start.2
  153.3 1.6 copy-start.3
  174.7 20.9 %all-to-all-start.2 = ((bf16[8,128,512]{2,1,0:T(8,128)(2,1)}), bf16[8,128,512]{2,1,0:T(8,128)(2,1)}, u32[]{:S(2)}, u32[]{:S(2)}) async-start(bf16[8,128,512]{2,1,0:T(8,128)(2,1)} %bitcast.25), calls=%async_computation.2 | async-start | bytes 2097152 | tf_op jit(solution)/shard_map/all_to_all | solution.py:592

commit v2 on v1

--- a/solution.py
+++ b/solution.py
@@ -15,8 +15,9 @@
 BLOCK = 256
 LOG2E = 1.4426950408889634
 REACH = 3
-QB = 128
-KB = 256
+QB = 256
+KB = 512
+SUB = 256
 NEG = -1e30
 
 F32 = jnp.float32
@@ -35,115 +36,132 @@
     return lax.dot_general(a, b, (((0,), (0,)), ((), ())), preferred_element_type=F32)
 
 
-def attention_kernel(starts, first, qg, kv_all, out, kv, s_scr, gp_scr, m_scr, l_scr, c_scr, acc, sems):
+def attention_kernel(starts, first, qg, kv_all, out, kv, kt, turned, e_scr, gp_scr, tops, sems):
     i = pl.program_id(0)
-    rows = kv.shape[0] // (REACH + 1)
+    rows = kv_all.shape[0] // (REACH + 1)
     lead = REACH * rows
     docs = starts.shape[0]
+    heads = out.shape[1] // DH
 
     @pl.when(i == 0)
     def _():
-        c = pltpu.make_async_copy(kv_all, kv, sems.at[0])
+        c = pltpu.make_async_copy(kv_all, kv.at[pl.ds(KB, kv_all.shape[0]), :], sems.at[0])
         c.start()
+        kv[0:KB, :] = jnp.zeros((KB, 2 * DH), BF16)
         c.wait()
 
+        def turn(n, _):
+            at = pl.ds(pl.multiple_of(n * KB, KB), KB)
+            kt[:, at] = jnp.transpose(kv[at, 0:DH])
+            return 0
+
+        lax.fori_loop(0, kv.shape[0] // KB, turn, 0)
+
+    for h in range(2 * heads):
+        turned[h] = jnp.transpose(qg[:, h * DH : (h + 1) * DH])
+
     base = first[0] - lead
-    q0 = first[0] + i * QB
-    qcol = lead + i * QB + lax.broadcasted_iota(jnp.int32, (QB, 1), 0)
-    dcol = jnp.zeros((QB, 1), jnp.int32)
+    q0 = lead + i * QB
+    qrow = q0 + iota((1, QB), 1)
+    drow = jnp.zeros((1, QB), jnp.int32)
     low = jnp.int32(0)
+    high = jnp.int32(0)
     for j in range(docs):
-        st = starts[j]
+        st = starts[j] - base
         low = jnp.where(st <= q0, st, low)
-        dcol = jnp.where(st - base <= qcol, st - base, dcol)
-    first_block = (low - base) // KB
-    blocks = (lead + i * QB + QB - 1) // KB - first_block + 1
-    heads = out.shape[1] // DH
-    q = jnp.concatenate([qg[:, h * DH : (h + 1) * DH] for h in range(heads)], axis=0)
-    g = jnp.concatenate([qg[:, (heads + h) * DH : (heads + h + 1) * DH] for h in range(heads)], axis=0)
-    m_scr[...] = jnp.full(m_scr.shape, NEG, F32)
-    l_scr[...] = jnp.zeros(l_scr.shape, F32)
-    c_scr[...] = jnp.zeros(c_scr.shape, F32)
-    acc[...] = jnp.zeros(acc.shape, F32)
-
-    def scores(b, _):
-        r0 = pl.multiple_of((first_block + b) * KB, KB)
-        k = kv[pl.ds(r0, KB), 0:DH]
-        v = kv[pl.ds(r0, KB), DH : 2 * DH]
-        key = r0 + lax.broadcasted_iota(jnp.int32, (QB, KB), 1)
-        ok = (key >= dcol) & (key <= qcol)
-        s = dot_nt(q, k)
-        gp_scr[b] = dot_nt(g, v)
+        high = jnp.where(st <= q0 + QB - 1, st, high)
+        drow = jnp.where(st <= qrow, st, drow)
+    end = q0 + QB
+    blocks = (end - low + KB - 1) // KB
+    begin = end - blocks * KB
+    edge = blocks - 1
+    full = jnp.minimum((high - begin + KB - 1) // KB, edge)
+    scale = DH**-0.5 * LOG2E
+
+    def fold(x):
+        return x.reshape(-1, 8, QB)
+
+    def place(b, n):
+        return pl.ds(pl.multiple_of(KB + begin + b * KB + n * SUB, 128), SUB)
+
+    def forward(masked, b, carry):
+        new = []
         for h in range(heads):
-            sh = jnp.where(ok, s[h * QB : (h + 1) * QB], NEG)
-            s_scr[b, h * QB : (h + 1) * QB, :] = sh
-            top = m_scr[h * QB : (h + 1) * QB, :]
-            for n in range(KB // 128):
-                top = jnp.maximum(top, sh[:, n * 128 : (n + 1) * 128])
-            m_scr[h * QB : (h + 1) * QB, :] = top
-        return 0
-
-    lax.fori_loop(0, blocks, scores, 0)
-    scale = DH**-0.5 * LOG2E
-    peak = jnp.max(m_scr[...], axis=1, keepdims=True)
-
-    def weights(b, _):
-        e = jnp.exp2((s_scr[b] - peak) * scale)
-        s_scr[b] = e
-        eg = e * gp_scr[b]
-        l = l_scr[...]
-        c = c_scr[...]
-        for n in range(KB // 128):
-            l += e[:, n * 128 : (n + 1) * 128]
-            c += eg[:, n * 128 : (n + 1) * 128]
-        l_scr[...] = l
-        c_scr[...] = c
-        return 0
-
-    lax.fori_loop(0, blocks, weights, 0)
-    total = jnp.sum(l_scr[...], axis=1, keepdims=True)
-    centre = jnp.sum(c_scr[...], axis=1, keepdims=True) / total
-
-    def grads(b, _):
-        r0 = pl.multiple_of((first_block + b) * KB, KB)
-        k = kv[pl.ds(r0, KB), 0:DH]
-        ds = (s_scr[b] * (gp_scr[b] - centre)).astype(BF16)
-        acc[...] += dot_nn(ds, k)
-        return 0
-
-    lax.fori_loop(0, blocks, grads, 0)
-    res = (acc[...] * (DH**-0.5 / total)).astype(BF16)
+            top, total, mean = carry[h]
+            for n in range(KB // SUB):
+                at = place(b, n)
+                s = dot_nn(kv[at, 0:DH], turned[h])
+                if masked:
+                    key = begin + b * KB + n * SUB + iota((SUB, QB), 0)
+                    s = jnp.where((key >= drow) & (key <= qrow), s, NEG)
+                last = top
+                top = jnp.maximum(top, jnp.max(jnp.max(fold(s), axis=0), axis=0, keepdims=True))
+                e = jnp.exp2((s - top) * scale)
+                gp = dot_nn(kv[at, DH : 2 * DH], turned[heads + h])
+                part = slice(n * SUB, (n + 1) * SUB)
+                e_scr[b, h, part, :] = e
+                gp_scr[b, h, part, :] = gp
+                tops[b, h, n] = jnp.broadcast_to(top, (8, QB))
+                fade = jnp.exp2((last - top) * scale)
+                total = total * fade + jnp.sum(fold(e), axis=0)
+                mean = mean * fade + jnp.sum(fold(e * gp), axis=0)
+            new.append((top, total, mean))
+        return tuple(new)
+
+    zero = jnp.zeros((8, QB), F32)
+    carry = ((jnp.full((1, QB), NEG, F32), zero, zero),) * heads
+    carry = lax.fori_loop(0, full, functools.partial(forward, True), carry)
+    carry = lax.fori_loop(full, edge, functools.partial(forward, False), carry)
+    carry = forward(True, edge, carry)
+    peak = [c[0] for c in carry]
+    total = [jnp.sum(c[1], axis=0, keepdims=True) for c in carry]
+    centre = [jnp.sum(c[2], axis=0, keepdims=True) / t for c, t in zip(carry, total)]
+
+    def grads(b, accs):
+        new = []
+        for h in range(heads):
+            acc = accs[h]
+            for n in range(KB // SUB):
+                part = slice(n * SUB, (n + 1) * SUB)
+                ds = (e_scr[b, h, part, :] * (gp_scr[b, h, part, :] - centre[h])).astype(BF16)
+                fade = jnp.exp2((tops[b, h, n, 0:1, :] - peak[h]) * scale)
+                acc += dot_nn(kt[:, place(b, n)], ds) * fade
+            new.append(acc)
+        return tuple(new)
+
+    accs = lax.fori_loop(0, blocks, grads, (jnp.zeros((DH, QB), F32),) * heads)
     for h in range(heads):
-        out[:, h * DH : (h + 1) * DH] = res[h * QB : (h + 1) * QB]
+        res = accs[h] * (DH**-0.5 / total[h])
+        out[:, h * DH : (h + 1) * DH] = jnp.transpose(res).astype(BF16)
 
 
 def attention(qg, kv, starts, first):
     rows = qg.shape[0]
     heads = qg.shape[1] // (2 * DH)
     lead = REACH * rows
-    most = (lead + QB) // KB + 2
-    hq = heads * QB
+    most = (lead + QB - 1 + KB - 1) // KB
     return pl.pallas_call(
         attention_kernel,
         grid_spec=pltpu.PrefetchScalarGridSpec(
             num_scalar_prefetch=2,
             grid=(rows // QB,),
-            in_specs=[pl.BlockSpec((QB, qg.shape[1]), lambda i, *_: (i, 0))]
-            + [pl.BlockSpec(memory_space=pltpu.HBM)],
+            in_specs=[
+                pl.BlockSpec((QB, qg.shape[1]), lambda i, *_: (i, 0)),
+                pl.BlockSpec(memory_space=pltpu.HBM),
+            ],
             out_specs=pl.BlockSpec((QB, heads * DH), lambda i, *_: (i, 0)),
             scratch_shapes=[
-                pltpu.VMEM((lead + rows, 2 * DH), BF16),
-                pltpu.VMEM((most, hq, KB), F32),
-                pltpu.VMEM((most, hq, KB), F32),
-                pltpu.VMEM((hq, 128), F32),
-                pltpu.VMEM((hq, 128), F32),
-                pltpu.VMEM((hq, 128), F32),
-                pltpu.VMEM((hq, DH), F32),
+                pltpu.VMEM((KB + lead + rows, 2 * DH), BF16),
+                pltpu.VMEM((DH, KB + lead + rows), BF16),
+                pltpu.VMEM((2 * heads, DH, QB), BF16),
+                pltpu.VMEM((most, heads, KB, QB), F32),
+                pltpu.VMEM((most, heads, KB, QB), F32),
+                pltpu.VMEM((most, heads, KB // SUB, 8, QB), F32),
                 pltpu.SemaphoreType.DMA((1,)),
             ],
         ),
         out_shape=jax.ShapeDtypeStruct((rows, heads * DH), BF16),
-        compiler_params=pltpu.CompilerParams(vmem_limit_bytes=56 << 20),
+        compiler_params=pltpu.CompilerParams(vmem_limit_bytes=58 << 20),
         cost_estimate=pl.CostEstimate(flops=12 * 10**9, bytes_accessed=6 << 20, transcendentals=16 * 10**6),
         name="attention",
     )(starts, first, qg, kv)
@@ -324,8 +342,6 @@
         c = remote(ends_send.at[d - 1], ends.at[hx], ends_ssem.at[d], ends_rsem.at[d], {"hx": to})
         c.start()
         end_moves.append(c)
-    for c in qg_moves:
-        c.start()
     make_ends(hx, ends.at[hx])
 
     for c in kv_own:
@@ -344,6 +360,8 @@
 
     for c in end_moves:
         c.wait_recv()
+    for c in qg_moves:
+        c.start()
     for n in range(chips):
         lk[n] = links_of(ends[n, 2 * columns :, :])
     prods = [None, lk[0]]
@@ -479,16 +497,71 @@
 ]
 
 
-def grads_kernel(starts, first, core, x, g, w, r, st, rates, skips, both, out_x, out_w, out_r, cum, cum_t, entering, to_end):
+def last_kernel(
+    starts, x, g, w, r, st, rates, skips, both, grad_q, out_x, out_w, out_r, out_q,
+    cum, cum_t, entering, to_end, res_x, res_w, res_r, own_sem, pair_send, pair_recv, q_send, q_recv,
+):
     j = pl.program_id(0)
+    ctx, hx, core = lax.axis_index("ctx"), lax.axis_index("hx"), lax.axis_index("core")
+    chips, cores = lax.axis_size("hx"), lax.axis_size("core")
+    parts = chips * cores
+    me = hx * cores + core
+    other = 1 - core
+    tokens = out_x.shape[0]
     columns = x.shape[1]
     heads = columns // HD
-    edge_scratch(starts, first, st, rates, cum, cum_t, entering, to_end)
-    begin = first[0]
+    qw = grad_q.shape[1]
+    begin = ctx * tokens * parts + hx * BLOCK
+    group = core * chips + j
+
+    def cols(n, width):
+        return pl.ds(pl.multiple_of(n * width, 128), width)
+
+    def remote(src, dst, ssem, rsem, device):
+        return pltpu.make_async_remote_copy(
+            src_ref=src, dst_ref=dst, send_sem=ssem, recv_sem=rsem, device_id=device, device_id_type=MESH
+        )
+
+    def q_moves():
+        moves = []
+        for d in range(1, parts):
+            p = lax.rem(me + d, parts)
+            device = {"hx": p // cores, "core": lax.rem(p, cores)}
+            moves.append(remote(grad_q.at[cols(p, tokens), :], out_q.at[:, cols(me, qw)], q_send.at[d], q_recv.at[d], device))
+        own = pltpu.make_async_copy(grad_q.at[cols(me, tokens), :], out_q.at[:, cols(me, qw)], own_sem.at[chips, 0])
+        return moves, own
+
+    def pair_moves(n):
+        moves, owns = [], []
+        for k, (res, out, width) in enumerate(((res_x, out_x, columns), (res_w, out_w, NS), (res_r, out_r, NS))):
+            place = out.at[:, cols(core * chips + n, width)]
+            moves.append(
+                remote(res.at[n, cols(other, tokens), :], place, pair_send.at[n, k], pair_recv.at[n, k], {"core": other})
+            )
+            owns.append(pltpu.make_async_copy(res.at[n, cols(core, tokens), :], place, own_sem.at[n, k]))
+        return moves, owns
+
+    @pl.when(j == 0)
+    def _():
+        barrier = pltpu.get_barrier_semaphore()
+        for d in range(1, parts):
+            p = lax.rem(me + d, parts)
+            pl.semaphore_signal(
+                barrier, inc=1, device_id={"hx": p // cores, "core": lax.rem(p, cores)}, device_id_type=MESH
+            )
+        pl.semaphore_wait(barrier, parts - 1)
+        moves, own = q_moves()
+        for c in moves + [own]:
+            c.start()
+        a, b, c, _ = edges(starts, begin, 0, st[...], rates[...])
+        cum[...] = a
+        cum_t[...] = jnp.transpose(a)
+        entering[...] = b
+        to_end[...] = c
+
     doc_col = doc_of(starts, begin + iota((BLOCK, 1), 0))
     doc_row = doc_of(starts, begin + iota((1, BLOCK), 1))
     ok = (iota((BLOCK, BLOCK), 0) <= iota((BLOCK, BLOCK), 1)) & (doc_col == doc_row)
-    group = core[0] * pl.num_programs(0) + j
     spread = spread_matrix(columns, group)
     end_wide = widen(to_end[...], spread)
     iw = (x[...].astype(F32) * end_wide).astype(BF16)
@@ -505,11 +578,11 @@
     rows_t = cum_t[pl.ds(offset, heads), :]
     cols_all = jnp.transpose(jnp.concatenate([rows_t, jnp.zeros((128 - heads, BLOCK), F32)], axis=0))
     for p in range(heads // 2):
-        cols = slice(p * 2 * HD, (p + 1) * 2 * HD)
-        xp = x[:, cols]
-        gp = g[:, cols]
+        at = slice(p * 2 * HD, (p + 1) * 2 * HD)
+        xp = x[:, at]
+        gp = g[:, at]
         zero = jnp.zeros_like(xp)
-        inner = skips[:, cols] * gp.astype(F32) + end_wide[:, cols] * carried[:, cols]
+        inner = skips[:, at] * gp.astype(F32) + end_wide[:, at] * carried[:, at]
         for half in range(2):
             h = 2 * p + half
             mine = lane if half == 0 else ~lane
@@ -517,18 +590,49 @@
             joint += decay * dot_nt(jnp.where(mine, xp, zero), gp)
             mixing = (scores * decay).astype(BF16)
             inner += dot_nn(mixing, jnp.where(mine, gp, zero))
-        out_x[:, cols] = inner.astype(BF16)
+        res_x[j, :, at] = inner.astype(BF16)
     low = joint.astype(BF16)
-    out_w[...] = (dot_nn(low, rv) + dot_nn(iw, back)).astype(BF16)
-    out_r[...] = (dot_tn(low, wv) + dot_nn(gw, state)).astype(BF16)
-
-
-def mixer_grads(mix, rates, skips, both, starts, first, core, columns, groups):
+    res_w[j] = (dot_nn(low, rv) + dot_nn(iw, back)).astype(BF16)
+    res_r[j] = (dot_tn(low, wv) + dot_nn(gw, state)).astype(BF16)
+
+    for n in range(chips):
+
+        @pl.when(j == n)
+        def _():
+            moves, owns = pair_moves(n)
+            for c in moves + owns:
+                c.start()
+
+    @pl.when(j == chips - 1)
+    def _():
+        moves, own = q_moves()
+        own.wait()
+        for c in moves:
+            c.wait_recv()
+        for c in moves:
+            c.wait_send()
+        for n in range(chips):
+            moves, owns = pair_moves(n)
+            for c in owns:
+                c.wait()
+            for c in moves:
+                c.wait_recv()
+            for c in moves:
+                c.wait_send()
+
+
+def last_stage(mix, rates, skips, both, starts, grad_q, parts, cores):
+    chips = both.shape[0]
+    columns = both.shape[1] // 2
+    tokens = BLOCK // cores
+    groups = chips * cores
+    hbm = pl.BlockSpec(memory_space=pltpu.HBM)
+    dma = pltpu.SemaphoreType.DMA
     return pl.pallas_call(
-        grads_kernel,
+        last_kernel,
         grid_spec=pltpu.PrefetchScalarGridSpec(
-            num_scalar_prefetch=3,
-            grid=(groups,),
+            num_scalar_prefetch=1,
+            grid=(chips,),
             in_specs=[
                 pl.BlockSpec((BLOCK, columns), lambda j, *_: (0, j)),
                 pl.BlockSpec((BLOCK, columns), lambda j, *_: (0, j)),
@@ -538,27 +642,31 @@
                 pl.BlockSpec((1, 128), lambda j, *_: (0, 0)),
                 pl.BlockSpec((1, columns), lambda j, *_: (0, j)),
                 pl.BlockSpec((1, 2 * columns, NS), lambda j, *_: (j, 0, 0)),
+                hbm,
             ],
-            out_specs=[
-                pl.BlockSpec((BLOCK, columns), lambda j, *_: (0, j)),
-                pl.BlockSpec((BLOCK, NS), lambda j, *_: (0, j)),
-                pl.BlockSpec((BLOCK, NS), lambda j, *_: (0, j)),
+            out_specs=[hbm] * 4,
+            scratch_shapes=EDGES
+            + [
+                pltpu.VMEM((chips, BLOCK, columns), BF16),
+                pltpu.VMEM((chips, BLOCK, NS), BF16),
+                pltpu.VMEM((chips, BLOCK, NS), BF16),
+                dma((chips + 1, 3)),
+                dma((chips, 3)),
+                dma((chips, 3)),
+                dma((parts,)),
+                dma((parts,)),
             ],
-            scratch_shapes=EDGES,
         ),
         out_shape=[
-            jax.ShapeDtypeStruct((BLOCK, groups * columns), BF16),
-            jax.ShapeDtypeStruct((BLOCK, groups * NS), BF16),
-            jax.ShapeDtypeStruct((BLOCK, groups * NS), BF16),
+            jax.ShapeDtypeStruct((tokens, groups * columns), BF16),
+            jax.ShapeDtypeStruct((tokens, groups * NS), BF16),
+            jax.ShapeDtypeStruct((tokens, groups * NS), BF16),
+            jax.ShapeDtypeStruct((tokens, parts * grad_q.shape[1]), BF16),
         ],
-        compiler_params=pltpu.CompilerParams(vmem_limit_bytes=40 << 20),
+        compiler_params=pltpu.CompilerParams(vmem_limit_bytes=56 << 20, collective_id=1, has_side_effects=True),
         cost_estimate=pl.CostEstimate(flops=8 * 10**9, bytes_accessed=14 << 20, transcendentals=5 * 10**6),
-        name="mixer_grads",
-    )(starts, first, core, *mix, rates, skips, both)
-
-
-def unpack(moved):
-    return moved.transpose(1, 0, 2).reshape(moved.shape[1], -1)
+        name="last_stage",
+    )(starts, *mix, rates, skips, both, grad_q)
 
 
 HEAD = ("hx", "core")
@@ -576,34 +684,17 @@
     slab = (lax.axis_index("ctx") * rows).astype(jnp.int32)
     starts = (jnp.cumsum(doc_lengths) - doc_lengths).astype(jnp.int32)
     slab_first = slab.reshape(1)
-    chip_first = (slab + lax.axis_index("hx") * BLOCK).astype(jnp.int32).reshape(1)
 
     slow = jnp.any(jnp.arange(MH, dtype=jnp.int32)[:, None] == slow_heads[None, :], axis=1)
     rates = jnp.where(slow, 1.0 / total_rows, fast_rates) * -LOG2E
     rates = rates.reshape(1, MH)
-    core = lax.axis_index("core").astype(jnp.int32).reshape(1)
     skips = lax.dynamic_slice_in_dim(skip_gains, lax.axis_index("core") * local_heads, local_heads)
     skips = jnp.repeat(skips, HD).reshape(1, local_heads * HD)
 
     *mix, kv, qg, both = first_stage(starts, x, grad, w, r, steps, q, k, v, ag, rates, parts, cores)
     both = lax.all_to_all(both, "hx", split_axis=0, concat_axis=0, tiled=True)
     grad_q = attention(qg, kv, starts, slab_first)
-    grad_q, both = lax.optimization_barrier((grad_q, both))
-    moved = lax.all_to_all(grad_q, HEAD, split_axis=0, concat_axis=0, tiled=True)
-    grad_q = unpack(moved.reshape(parts, tokens, -1))
-
-    gx, gw, gr = mixer_grads(mix, rates, skips, both, starts, chip_first, core, columns, chips)
-    joined = jnp.concatenate([gx, gw, gr], axis=1)
-    moved = lax.all_to_all(joined, "core", split_axis=0, concat_axis=0, tiled=True)
-    moved = moved.reshape(cores, tokens, -1)
-    wide = local_heads * HD
-    thin = chips * NS
-    return (
-        unpack(moved[:, :, :wide]),
-        unpack(moved[:, :, wide : wide + thin]),
-        unpack(moved[:, :, wide + thin :]),
-        grad_q,
-    )
+    return tuple(last_stage(mix, rates, skips, both, starts, grad_q, parts, cores))
 
 
 def solution(mesh):

time: 198 us -> 153 us (0.77)
  Pallas kernels: 157 us -> 136 us
  waiting for transfers between devices: 13 us -> 0.01 us
  blocking collectives: 5.84 us -> 0 us
  starting transfers between devices: 8.53 us -> 3.8 us
    pallas_call x1, Pallas kernels: 66.7 us -> 39 us  [attention(): pl.pallas_call(attention_kernel, grid_spec=pltpu.PrefetchScalarGridSpec(n...]
    all_to_all x1 -> x0, waiting for transfers between devices: 13 us -> none  [shards(): lax.all_to_all(grad_q, HEAD, split_axis=0, concat_axis=0, tiled=True)]
    pallas_call x1, Pallas kernels: 13.7 us -> 20.8 us  [last_stage(): pl.pallas_call(last_kernel, grid_spec=pltpu.PrefetchScalarGridSpec(num_sc...]
    all_to_all x1 -> x0, blocking collectives: 5.84 us -> none  [shards(): lax.all_to_all(joined, 'core', split_axis=0, concat_axis=0, tiled=True)]
    reshape x4 -> x0, local copies, waits for them, and re-layouts: 5.22 us -> none  [unpack(): return moved.transpose(1, 0, 2).reshape(moved.shape[1], -1)]
    all_to_all x1 -> x0, starting transfers between devices: 4.81 us -> none  [shards(): lax.all_to_all(grad_q, HEAD, split_axis=0, concat_axis=0, tiled=True)]
    unnamed x18 -> x14, local copies, waits for them, and re-layouts: 3.37 us -> 6.92 us
  transfers between devices with their start and end apart: 2 -> 1, of which waited for: 1 -> 0; matrix products, arithmetic and copies ran while one was open for 2% -> 1% of each run, Pallas kernels for 34% -> 26%
where the time goes in v2:
time: 153 us
  Pallas kernels  136 us (89%)
  local copies, waits for them, and re-layouts  8.5 us (6%)
  starting transfers between devices  3.8 us (2%)
  other arithmetic  3.26 us (2%)
    pallas_call x1, Pallas kernels, first_stage(): pl.pallas_call(first_kernel, in_specs=[pl.BlockSpec(memory_space=pltpu.SM...  76.5 us
    pallas_call x1, Pallas kernels, attention(): pl.pallas_call(attention_kernel, grid_spec=pltpu.PrefetchScalarGridSpec(n...  39 us
    pallas_call x1, Pallas kernels, last_stage(): pl.pallas_call(last_kernel, grid_spec=pltpu.PrefetchScalarGridSpec(num_sc...  20.8 us
    unnamed x14, local copies, waits for them, and re-layouts  6.92 us
    all_to_all x1, starting transfers between devices, shards(): both = lax.all_to_all(both, 'hx', split_axis=0, concat_axis=0, tiled=True)  3.8 us
  transfers between devices with their start and end apart: 1, of which 0 were waited for; matrix products, arithmetic and copies ran while one was open for 1% of the time, Pallas kernels for 26%

profile of v2, /device:TPU:128, one launch (start us, length us, event | category | flops | bytes accessed | tf_op | source)
XLA Modules:
  0.0 152.6 jit_solution(4639546845012153056)
XLA Ops:
  0.6 0.7 copy.19
  1.4 0.1 reduce
  1.5 1.2 sub.3.starts
  2.7 0.7 fusion
  3.4 1.2 multiply_bitcast_fusion.rates
  4.6 76.5 %first_stage.1 = (bf16[256,4096]{1,0:T(8,128)(2,1)}, bf16[256,4096]{1,0:T(8,128)(2,1)}, bf16[256,512]{1,0:T(8,128)(2,1)}, bf16[256,512]{1,0:T(8,128)(2,1)}, bf16...) custom-call(s32[16]{0:T(128)} %sub.3.starts, ...), custom_call_target="tpu_custom_call" | custom-call | flops 2000000000 | bytes 16777216 | tf_op jit(solution)/shard_map/first_stage/pallas_call | solution.py:446
  81.1 0.0 copy-start.4
  81.1 3.8 %all-to-all-start = ((bf16[4,2048,128]{2,1,0:T(8,128)(2,1)}), bf16[4,2048,128]{2,1,0:T(8,128)(2,1)S(1)}, u32[]{:S(2)}, u32[]{:S(2)}) async-start(bf16[4,2048,128]{2,1,0:T(8,128)(2,1)} %get-tuple-element.17), calls=%async_computation | async-start | bytes 4194304 | tf_op jit(solution)/shard_map/all_to_all | solution.py:695
  84.9 0.0 copy-done.4
  84.9 0.1 dynamic_slice.3
  85.0 0.1 broadcast_in_dim.10
  85.1 0.7 reshape_reshape.3.skips
  85.8 39.0 %attention.1.grad_q = bf16[1024,512]{1,0:T(8,128)(2,1)} custom-call(s32[16]{0:T(128)} %sub.3.starts, s32[1]{0:T(128)} %bitcast.2.first, bf16[1024,1024]{1,0:T(8,128)(2,1)} %get-tuple-element.18.qg, bf16[4096,256]{1,0:T(8,128)(2,1)} %get-tuple-element.19.kv_all), custom_call_target="tpu_custom_call" | custom-call | flops 12000000000 | bytes 6291456 | tf_op jit(solution)/shard_map/attention/pallas_call | solution.py:143
  124.8 0.0 all-to-all-done.both
  124.8 0.0 copy-start
  124.9 1.3 copy-done
  126.2 20.8 %last_stage.1 = (bf16[128,8192]{1,0:T(8,128)(2,1)}, bf16[128,1024]{1,0:T(8,128)(2,1)}, bf16[128,1024]{1,0:T(8,128)(2,1)}, bf16[128,4096]{1,0:T(8,128)(2,1)}) custom-call(s32[16]{0:T(128)} %sub.3.starts, bf16[256,4096]{1,0:T(8,128)(2,1)} %get-tuple-element.12.x, bf16[256,4096]{1,0:T(8,128)(2,1)} %get-tuple-element.13.g, ...), custom_call_target="tpu_custom_call" | custom-call | flops 8000000000 | bytes 14680064 | tf_op jit(solution)/shard_map/last_stage/pallas_call | solution.py:631
  147.0 0.0 copy-start.3
  147.0 0.0 copy-start.2
  147.0 0.0 copy-start.1
  147.0 3.2 %copy.24 = bf16[128,8192]{1,0:T(8,128)(2,1)} copy(bf16[128,8192]{1,0:T(8,128)(2,1)} %get-tuple-element.24) | data formatting | bytes 4194304
  150.2 0.0 copy-done.3
  150.2 0.7 copy.25
  150.9 0.0 copy-done.2
  150.9 0.7 copy.26
  151.6 0.0 copy-done.1
  151.6 1.0 copy.27
  (1 shorter events, 0.0 us)
Async XLA Ops:
  81.1 3.8 %copy-start.4 = (f32[128]{0:T(128)S(1)}, f32[128]{0:T(128)}, u32[]{:S(2)}) copy-start(f32[128]{0:T(128)} %param.19) | copy-start | bytes 1540
  81.1 43.7 %all-to-all-start = ((bf16[4,2048,128]{2,1,0:T(8,128)(2,1)}), bf16[4,2048,128]{2,1,0:T(8,128)(2,1)S(1)}, u32[]{:S(2)}, u32[]{:S(2)}) async-start(bf16[4,2048,128]{2,1,0:T(8,128)(2,1)} %get-tuple-element.17), calls=%async_computation | async-start | bytes 4194304 | tf_op jit(solution)/shard_map/all_to_all | solution.py:695
  124.8 1.3 copy-start
  147.0 3.2 %copy-start.3 = (bf16[128,1024]{1,0:T(8,128)(2,1)S(1)}, bf16[128,1024]{1,0:T(8,128)(2,1)}, u32[]{:S(2)}) copy-start(bf16[128,1024]{1,0:T(8,128)(2,1)} %get-tuple-element.25) | copy-start | bytes 786436
  147.0 3.9 %copy-start.2 = (bf16[128,1024]{1,0:T(8,128)(2,1)S(1)}, bf16[128,1024]{1,0:T(8,128)(2,1)}, u32[]{:S(2)}) copy-start(bf16[128,1024]{1,0:T(8,128)(2,1)} %get-tuple-element.26) | copy-start | bytes 786436
  147.0 4.6 %copy-start.1 = (bf16[128,4096]{1,0:T(8,128)(2,1)S(1)}, bf16[128,4096]{1,0:T(8,128)(2,1)}, u32[]{:S(2)}) copy-start(bf16[128,4096]{1,0:T(8,128)(2,1)} %get-tuple-element.27) | copy-start | bytes 3145732

commit v3 on v2

--- a/solution.py
+++ b/solution.py
@@ -18,6 +18,7 @@
 QB = 256
 KB = 512
 SUB = 256
+EARLY = 3
 NEG = -1e30
 
 F32 = jnp.float32
@@ -36,11 +37,10 @@
     return lax.dot_general(a, b, (((0,), (0,)), ((), ())), preferred_element_type=F32)
 
 
-def attention_kernel(starts, first, qg, kv_all, out, kv, kt, turned, e_scr, gp_scr, tops, sems):
+def attention_kernel(lengths, first, qg, kv_all, out, kv, kt, turned, e_scr, gp_scr, tops, sems):
     i = pl.program_id(0)
     rows = kv_all.shape[0] // (REACH + 1)
     lead = REACH * rows
-    docs = starts.shape[0]
     heads = out.shape[1] // DH
 
     @pl.when(i == 0)
@@ -66,8 +66,8 @@
     drow = jnp.zeros((1, QB), jnp.int32)
     low = jnp.int32(0)
     high = jnp.int32(0)
-    for j in range(docs):
-        st = starts[j] - base
+    for start in starts_of(lengths):
+        st = start - base
         low = jnp.where(st <= q0, st, low)
         high = jnp.where(st <= q0 + QB - 1, st, high)
         drow = jnp.where(st <= qrow, st, drow)
@@ -135,7 +135,7 @@
         out[:, h * DH : (h + 1) * DH] = jnp.transpose(res).astype(BF16)
 
 
-def attention(qg, kv, starts, first):
+def attention(qg, kv, lengths, first):
     rows = qg.shape[0]
     heads = qg.shape[1] // (2 * DH)
     lead = REACH * rows
@@ -164,7 +164,7 @@
         compiler_params=pltpu.CompilerParams(vmem_limit_bytes=58 << 20),
         cost_estimate=pl.CostEstimate(flops=12 * 10**9, bytes_accessed=6 << 20, transcendentals=16 * 10**6),
         name="attention",
-    )(starts, first, qg, kv)
+    )(lengths, first, qg, kv)
 
 
 def split_sum(tri, dl):
@@ -179,10 +179,25 @@
     return lax.broadcasted_iota(jnp.int32, shape, dim)
 
 
+def starts_of(lengths):
+    starts = [jnp.int32(0)]
+    for j in range(lengths.shape[0] - 1):
+        starts.append(starts[-1] + lengths[j])
+    return starts
+
+
+def rates_of(slow, fast, total_rows):
+    rates = fast[...]
+    lane = iota(rates.shape, 1)
+    for n in range(slow.shape[0]):
+        rates = jnp.where(lane == slow[n], 1.0 / total_rows, rates)
+    return rates * -LOG2E
+
+
 def doc_of(starts, pos):
     d = jnp.zeros(pos.shape, jnp.int32)
-    for j in range(starts.shape[0]):
-        d += (starts[j] <= pos).astype(jnp.int32)
+    for st in starts:
+        d += (st <= pos).astype(jnp.int32)
     return d
 
 
@@ -228,7 +243,7 @@
 
 
 def first_kernel(
-    starts, x, g, w, r, st, q, k, v, ag, rates,
+    lengths, slow, x, g, w, r, st, q, k, v, ag, fast,
     xs_out, gs_out, ws_out, rs_out, st_out, kv, qg, both,
     xs, gs, ws, rs, sts, ends_send, ends, lk, state, back, fs, fr, bs, br,
     own_sem, pair_send, pair_recv, head_send, head_recv, ends_ssem, ends_rsem, ring_ssem, ring_rsem, out_sem,
@@ -246,6 +261,7 @@
     columns = half // chips
     heads = columns // HD
     begin = ctx * rows + hx * BLOCK
+    starts = starts_of(lengths)
 
     def peer(d):
         p = lax.rem(me + d, parts)
@@ -297,7 +313,7 @@
                 remote(src.at[:, cols(p, width)], dst.at[at, place], head_send.at[n, d], head_recv.at[n, d], device)
             )
         own.append(pltpu.make_async_copy(src.at[:, cols(me, width)], dst.at[at, place], own_sem.at[5 + n]))
-    for c in kv_moves + kv_own + qg_own:
+    for c in kv_moves + kv_own + qg_own + qg_moves[:EARLY]:
         c.start()
 
     for c in owns:
@@ -311,7 +327,7 @@
     for c in outs:
         c.start()
 
-    cum, entering, to_end, linked = edges(starts, begin, 0, sts[...], rates[...])
+    cum, entering, to_end, linked = edges(starts, begin, 0, sts[...], rates_of(slow, fast, rows * slabs))
     entering_hi = entering.astype(BF16)
     entering_lo = (entering - entering_hi.astype(F32)).astype(BF16)
     to_end_hi = to_end.astype(BF16)
@@ -335,6 +351,12 @@
         out[2 * columns : 2 * columns + heads, :] = hi
         out[2 * columns + heads : 2 * columns + 2 * heads, :] = (link - hi.astype(F32)).astype(BF16)
 
+    hops = []
+    for n in range(REACH):
+        src = pl.ds((REACH - n) * rows, rows)
+        dst = pl.ds((REACH - n - 1) * rows, rows)
+        hops.append(remote(kv.at[src, :], kv.at[dst, :], ring_ssem.at[n], ring_rsem.at[n], after))
+
     end_moves = []
     for d in range(1, chips):
         to = lax.rem(hx + d, chips)
@@ -342,25 +364,20 @@
         c = remote(ends_send.at[d - 1], ends.at[hx], ends_ssem.at[d], ends_rsem.at[d], {"hx": to})
         c.start()
         end_moves.append(c)
+        if d == 2:
+            for c in kv_own:
+                c.wait()
+            for c in kv_moves:
+                c.wait_recv()
+            hops[0].start()
     make_ends(hx, ends.at[hx])
 
-    for c in kv_own:
-        c.wait()
-    for c in kv_moves:
-        c.wait_recv()
-    hops = []
-    for n in range(REACH):
-        src = pl.ds((REACH - n) * rows, rows)
-        dst = pl.ds((REACH - n - 1) * rows, rows)
-        hops.append(remote(kv.at[src, :], kv.at[dst, :], ring_ssem.at[n], ring_rsem.at[n], after))
-    for n in range(REACH):
-        if n > 0:
-            hops[n - 1].wait_recv()
-        hops[n].start()
+    hops[0].wait_recv()
+    hops[1].start()
 
     for c in end_moves:
         c.wait_recv()
-    for c in qg_moves:
+    for c in qg_moves[EARLY:]:
         c.start()
     for n in range(chips):
         lk[n] = links_of(ends[n, 2 * columns :, :])
@@ -388,25 +405,42 @@
         bs[0, at, :] = b.astype(BF16)
         return 0
 
-    lax.fori_loop(0, heads, totals, 0)
-    fwd = [remote(fs.at[n], fr.at[n], ring_ssem.at[3 + n], ring_rsem.at[3 + n], after) for n in range(REACH)]
-    bwd = [remote(bs.at[n], br.at[n], ring_ssem.at[6 + n], ring_rsem.at[6 + n], ahead) for n in range(REACH)]
-    fwd[0].start()
-    bwd[0].start()
+    def ring(src, dst, sem, device):
+        moves = []
+        for n in range(REACH):
+            pair = []
+            for part in range(2):
+                at = pl.ds(part * columns // 2, columns // 2)
+                k = sem + 2 * n + part
+                pair.append(remote(src.at[n, at, :], dst.at[n, at, :], ring_ssem.at[k], ring_rsem.at[k], device))
+            moves.append(pair)
+        return moves
+
+    fwd = ring(fs, fr, REACH, after)
+    bwd = ring(bs, br, 3 * REACH, ahead)
+
+    def over(part, body):
+        lax.fori_loop(part * heads // 2, (part + 1) * heads // 2, body, 0)
+
+    for part in range(2):
+        over(part, totals)
+        fwd[0][part].start()
+        bwd[0][part].start()
+    hops[1].wait_recv()
+    hops[2].start()
     for n in range(1, REACH):
-        for moves, base, recv, send in ((bwd, back, br, bs), (fwd, state, fr, fs)):
-            moves[n - 1].wait_recv()
-
-            def step(h, _):
-                at, unused = head_rows(h)
-                val = base[at, :] + lk[whole, pl.ds(h, 1), :] * recv[n - 1, at, :].astype(F32)
-                send[n, at, :] = val.astype(BF16)
-                return 0
-
-            lax.fori_loop(0, heads, step, 0)
-            moves[n].start()
-    fwd[REACH - 1].wait_recv()
-    bwd[REACH - 1].wait_recv()
+        for part in range(2):
+            for moves, base, recv, send in ((bwd, back, br, bs), (fwd, state, fr, fs)):
+                moves[n - 1][part].wait_recv()
+
+                def step(h, _):
+                    at, unused = head_rows(h)
+                    val = base[at, :] + lk[whole, pl.ds(h, 1), :] * recv[n - 1, at, :].astype(F32)
+                    send[n, at, :] = val.astype(BF16)
+                    return 0
+
+                over(part, step)
+                moves[n][part].start()
 
     def chip_states(h, _):
         at, bt = head_rows(h)
@@ -421,17 +455,20 @@
             b = lk[n, one, :] * b + ends[n, bt, :].astype(F32)
         return 0
 
-    lax.fori_loop(0, heads, chip_states, 0)
+    for part in range(2):
+        bwd[REACH - 1][part].wait_recv()
+        fwd[REACH - 1][part].wait_recv()
+        over(part, chip_states)
     hops[REACH - 1].wait_recv()
     for c in qg_own + outs:
         c.wait()
     for c in qg_moves:
         c.wait_recv()
-    for c in pairs + kv_moves + qg_moves + end_moves + hops + fwd + bwd:
+    for c in pairs + kv_moves + qg_moves + end_moves + hops + sum(fwd + bwd, []):
         c.wait_send()
 
 
-def first_stage(starts, x, g, w, r, st, q, k, v, ag, rates, parts, cores):
+def first_stage(lengths, slow, x, g, w, r, st, q, k, v, ag, fast, parts, cores):
     chips = parts // cores
     tokens = x.shape[0]
     rows = tokens * parts
@@ -445,7 +482,7 @@
     dma = pltpu.SemaphoreType.DMA
     return pl.pallas_call(
         first_kernel,
-        in_specs=[pl.BlockSpec(memory_space=pltpu.SMEM)] + [hbm] * 9 + [vmem],
+        in_specs=[pl.BlockSpec(memory_space=pltpu.SMEM)] * 2 + [hbm] * 9 + [vmem],
         out_specs=[hbm] * 7 + [vmem],
         out_shape=[
             jax.ShapeDtypeStruct((both_rows, half), BF16),
@@ -479,14 +516,14 @@
             dma((4, parts)),
             dma((chips,)),
             dma((chips,)),
-            dma((9,)),
-            dma((9,)),
+            dma((REACH * 5,)),
+            dma((REACH * 5,)),
             dma((5,)),
         ],
         compiler_params=pltpu.CompilerParams(vmem_limit_bytes=60 << 20, collective_id=0, has_side_effects=True),
         cost_estimate=pl.CostEstimate(flops=2 * 10**9, bytes_accessed=16 << 20, transcendentals=10**5),
         name="first_stage",
-    )(starts, x, g, w, r, st, q, k, v, ag, rates)
+    )(lengths, slow, x, g, w, r, st, q, k, v, ag, fast)
 
 
 EDGES = [
@@ -498,7 +535,7 @@
 
 
 def last_kernel(
-    starts, x, g, w, r, st, rates, skips, both, grad_q, out_x, out_w, out_r, out_q,
+    lengths, slow, x, g, w, r, st, fast, gains, both, grad_q, out_x, out_w, out_r, out_q,
     cum, cum_t, entering, to_end, res_x, res_w, res_r, own_sem, pair_send, pair_recv, q_send, q_recv,
 ):
     j = pl.program_id(0)
@@ -513,6 +550,7 @@
     qw = grad_q.shape[1]
     begin = ctx * tokens * parts + hx * BLOCK
     group = core * chips + j
+    starts = starts_of(lengths)
 
     def cols(n, width):
         return pl.ds(pl.multiple_of(n * width, 128), width)
@@ -553,7 +591,7 @@
         moves, own = q_moves()
         for c in moves + [own]:
             c.start()
-        a, b, c, _ = edges(starts, begin, 0, st[...], rates[...])
+        a, b, c, _ = edges(starts, begin, 0, st[...], rates_of(slow, fast, tokens * parts * lax.axis_size("ctx")))
         cum[...] = a
         cum_t[...] = jnp.transpose(a)
         entering[...] = b
@@ -563,6 +601,7 @@
     doc_row = doc_of(starts, begin + iota((1, BLOCK), 1))
     ok = (iota((BLOCK, BLOCK), 0) <= iota((BLOCK, BLOCK), 1)) & (doc_col == doc_row)
     spread = spread_matrix(columns, group)
+    skips = widen(jnp.broadcast_to(gains[...], (8, 128)), spread)[0:1, :]
     end_wide = widen(to_end[...], spread)
     iw = (x[...].astype(F32) * end_wide).astype(BF16)
     gw = (g[...].astype(F32) * widen(entering[...], spread)).astype(BF16)
@@ -621,7 +660,7 @@
                 c.wait_send()
 
 
-def last_stage(mix, rates, skips, both, starts, grad_q, parts, cores):
+def last_stage(lengths, slow, mix, fast, gains, both, grad_q, parts, cores):
     chips = both.shape[0]
     columns = both.shape[1] // 2
     tokens = BLOCK // cores
@@ -631,7 +670,7 @@
     return pl.pallas_call(
         last_kernel,
         grid_spec=pltpu.PrefetchScalarGridSpec(
-            num_scalar_prefetch=1,
+            num_scalar_prefetch=2,
             grid=(chips,),
             in_specs=[
                 pl.BlockSpec((BLOCK, columns), lambda j, *_: (0, j)),
@@ -640,7 +679,7 @@
                 pl.BlockSpec((BLOCK, NS), lambda j, *_: (0, j)),
                 pl.BlockSpec((BLOCK, 128), lambda j, *_: (0, 0)),
                 pl.BlockSpec((1, 128), lambda j, *_: (0, 0)),
-                pl.BlockSpec((1, columns), lambda j, *_: (0, j)),
+                pl.BlockSpec((1, 128), lambda j, *_: (0, 0)),
                 pl.BlockSpec((1, 2 * columns, NS), lambda j, *_: (j, 0, 0)),
                 hbm,
             ],
@@ -666,7 +705,7 @@
         compiler_params=pltpu.CompilerParams(vmem_limit_bytes=56 << 20, collective_id=1, has_side_effects=True),
         cost_estimate=pl.CostEstimate(flops=8 * 10**9, bytes_accessed=14 << 20, transcendentals=5 * 10**6),
         name="last_stage",
-    )(starts, *mix, rates, skips, both, grad_q)
+    )(lengths, slow, *mix, fast, gains, both, grad_q)
 
 
 HEAD = ("hx", "core")
@@ -674,27 +713,14 @@
 
 def shards(x, w, r, steps, fast_rates, slow_heads, skip_gains, grad, q, k, v, ag, doc_lengths):
     parts = lax.axis_size(HEAD)
-    chips = lax.axis_size("hx")
     cores = lax.axis_size("core")
-    tokens = x.shape[0]
-    rows = tokens * parts
-    columns = x.shape[1] // parts
-    local_heads = MH // cores
-    total_rows = rows * lax.axis_size("ctx")
-    slab = (lax.axis_index("ctx") * rows).astype(jnp.int32)
-    starts = (jnp.cumsum(doc_lengths) - doc_lengths).astype(jnp.int32)
-    slab_first = slab.reshape(1)
-
-    slow = jnp.any(jnp.arange(MH, dtype=jnp.int32)[:, None] == slow_heads[None, :], axis=1)
-    rates = jnp.where(slow, 1.0 / total_rows, fast_rates) * -LOG2E
-    rates = rates.reshape(1, MH)
-    skips = lax.dynamic_slice_in_dim(skip_gains, lax.axis_index("core") * local_heads, local_heads)
-    skips = jnp.repeat(skips, HD).reshape(1, local_heads * HD)
-
-    *mix, kv, qg, both = first_stage(starts, x, grad, w, r, steps, q, k, v, ag, rates, parts, cores)
+    slab_first = (lax.axis_index("ctx") * x.shape[0] * parts).astype(jnp.int32).reshape(1)
+    fast = fast_rates.reshape(1, MH)
+    gains = skip_gains.reshape(1, MH)
+    *mix, kv, qg, both = first_stage(doc_lengths, slow_heads, x, grad, w, r, steps, q, k, v, ag, fast, parts, cores)
     both = lax.all_to_all(both, "hx", split_axis=0, concat_axis=0, tiled=True)
-    grad_q = attention(qg, kv, starts, slab_first)
-    return tuple(last_stage(mix, rates, skips, both, starts, grad_q, parts, cores))
+    grad_q = attention(qg, kv, doc_lengths, slab_first)
+    return tuple(last_stage(doc_lengths, slow_heads, mix, fast, gains, both, grad_q, parts, cores))
 
 
 def solution(mesh):

time: 153 us -> 152 us (level)
  the two profiles are of different devices: /device:TPU:128 before, /device:TPU:25 now
where the time goes in v3:
time: 152 us
  Pallas kernels  140 us (92%)
  local copies, waits for them, and re-layouts  6.91 us (5%)
  starting transfers between devices  3.8 us (2%)
    pallas_call x1, Pallas kernels, first_stage(): pl.pallas_call(first_kernel, in_specs=[pl.BlockSpec(memory_space=pltpu.SM...  80.1 us
    pallas_call x1, Pallas kernels, attention(): pl.pallas_call(attention_kernel, grid_spec=pltpu.PrefetchScalarGridSpec(n...  39 us
    pallas_call x1, Pallas kernels, last_stage(): pl.pallas_call(last_kernel, grid_spec=pltpu.PrefetchScalarGridSpec(num_sc...  21.2 us
    unnamed x12, local copies, waits for them, and re-layouts  6.91 us
    all_to_all x1, starting transfers between devices, shards(): both = lax.all_to_all(both, 'hx', split_axis=0, concat_axis=0, tiled=True)  3.8 us
  transfers between devices with their start and end apart: 1, of which 0 were waited for; matrix products, arithmetic and copies ran while one was open for 0% of the time, Pallas kernels for 26%

profile of v3, /device:TPU:25, one launch (start us, length us, event | category | flops | bytes accessed | tf_op | source)
XLA Modules:
  0.0 151.7 jit_solution(6322150584238975341)
XLA Ops:
  0.6 80.1 %first_stage.1 = (bf16[256,4096]{1,0:T(8,128)(2,1)}, bf16[256,4096]{1,0:T(8,128)(2,1)}, bf16[256,512]{1,0:T(8,128)(2,1)}, bf16[256,512]{1,0:T(8,128)(2,1)}, bf16...) custom-call(s32[16]{0:T(128)} %lengths.5, ...), custom_call_target="tpu_custom_call" | custom-call | flops 2000000000 | bytes 16777216 | tf_op jit(solution)/shard_map/first_stage/pallas_call | solution.py:483
  80.8 3.8 %all-to-all-start = ((bf16[4,2048,128]{2,1,0:T(8,128)(2,1)}), bf16[4,2048,128]{2,1,0:T(8,128)(2,1)S(1)}, u32[]{:S(2)}, u32[]{:S(2)}) async-start(bf16[4,2048,128]{2,1,0:T(8,128)(2,1)} %get-tuple-element.17), calls=%async_computation | async-start | bytes 4194304 | tf_op jit(solution)/shard_map/all_to_all | solution.py:721
  84.6 39.0 %attention.1.grad_q = bf16[1024,512]{1,0:T(8,128)(2,1)} custom-call(s32[16]{0:T(128)} %lengths.5, s32[1]{0:T(128)} %bitcast.2.first, bf16[1024,1024]{1,0:T(8,128)(2,1)} %get-tuple-element.18.qg, bf16[4096,256]{1,0:T(8,128)(2,1)} %get-tuple-element.19.kv_all), custom_call_target="tpu_custom_call" | custom-call | flops 12000000000 | bytes 6291456 | tf_op jit(solution)/shard_map/attention/pallas_call | solution.py:143
  123.6 0.0 all-to-all-done.both
  123.6 0.0 copy-start
  123.6 1.3 copy-done
  124.9 21.2 %last_stage.1 = (bf16[128,8192]{1,0:T(8,128)(2,1)}, bf16[128,1024]{1,0:T(8,128)(2,1)}, bf16[128,1024]{1,0:T(8,128)(2,1)}, bf16[128,4096]{1,0:T(8,128)(2,1)}) custom-call(s32[16]{0:T(128)} %lengths.5, s32[64]{0:T(128)} %slow.3, bf16[256,4096]{1,0:T(8,128)(2,1)} %get-tuple-element.12.x, bf16[256,4096]{1,0:T(8,128)(2,1)} %get-tuple-element.13.g, ...), custom_call_target="tpu_custom_call" | custom-call | flops 8000000000 | bytes 14680064 | tf_op jit(solution)/shard_map/last_stage/pallas_call | solution.py:670
  146.1 0.0 copy-start.3
  146.1 0.0 copy-start.2
  146.1 0.0 copy-start.1
  146.1 3.2 %copy.21 = bf16[128,8192]{1,0:T(8,128)(2,1)} copy(bf16[128,8192]{1,0:T(8,128)(2,1)} %get-tuple-element.24) | data formatting | bytes 4194304
  149.3 0.0 copy-done.3
  149.3 0.7 copy.22
  150.1 0.0 copy-done.2
  150.1 0.7 copy.23
  150.8 0.0 copy-done.1
  150.8 1.0 copy.24
Async XLA Ops:
  80.8 42.8 %all-to-all-start = ((bf16[4,2048,128]{2,1,0:T(8,128)(2,1)}), bf16[4,2048,128]{2,1,0:T(8,128)(2,1)S(1)}, u32[]{:S(2)}, u32[]{:S(2)}) async-start(bf16[4,2048,128]{2,1,0:T(8,128)(2,1)} %get-tuple-element.17), calls=%async_computation | async-start | bytes 4194304 | tf_op jit(solution)/shard_map/all_to_all | solution.py:721
  123.6 1.3 copy-start
  146.1 3.2 %copy-start.3 = (bf16[128,1024]{1,0:T(8,128)(2,1)S(1)}, bf16[128,1024]{1,0:T(8,128)(2,1)}, u32[]{:S(2)}) copy-start(bf16[128,1024]{1,0:T(8,128)(2,1)} %get-tuple-element.25) | copy-start | bytes 786436
  146.1 3.9 %copy-start.2 = (bf16[128,1024]{1,0:T(8,128)(2,1)S(1)}, bf16[128,1024]{1,0:T(8,128)(2,1)}, u32[]{:S(2)}) copy-start(bf16[128,1024]{1,0:T(8,128)(2,1)} %get-tuple-element.26) | copy-start | bytes 786436
  146.1 4.6 %copy-start.1 = (bf16[128,4096]{1,0:T(8,128)(2,1)S(1)}, bf16[128,4096]{1,0:T(8,128)(2,1)}, u32[]{:S(2)}) copy-start(bf16[128,4096]{1,0:T(8,128)(2,1)} %get-tuple-element.27) | copy-start | bytes 3145732

commit v4 on v3

--- a/solution.py
+++ b/solution.py
@@ -224,16 +224,6 @@
     return (iota((128, columns), 0) == group * (columns // HD) + iota((128, columns), 1) // HD).astype(BF16)
 
 
-def edge_scratch(starts, first, st, rates, cum, cum_t, entering, to_end):
-    @pl.when(pl.program_id(0) == 0)
-    def _():
-        a, b, c, _ = edges(starts, first[0], 0, st[...], rates[...])
-        cum[...] = a
-        cum_t[...] = jnp.transpose(a)
-        entering[...] = b
-        to_end[...] = c
-
-
 MESH = pl.DeviceIdType.MESH
 
 
@@ -243,9 +233,9 @@
 
 
 def first_kernel(
-    lengths, slow, x, g, w, r, st, q, k, v, ag, fast,
-    xs_out, gs_out, ws_out, rs_out, st_out, kv, qg, both,
-    xs, gs, ws, rs, sts, ends_send, ends, lk, state, back, fs, fr, bs, br,
+    lengths, slow, x, g, w, r, st, q, k, v, ag, fast, gains,
+    xs_out, gs_out, ws_out, st_out, ix_out, iw_out, ir_out, kv, qg, both,
+    xs, gs, ws, rs, sts, ix, iw_in, ir_in, cum_t, ends_send, ends, lk, state, back, fs, fr, bs, br,
     own_sem, pair_send, pair_recv, head_send, head_recv, ends_ssem, ends_rsem, ring_ssem, ring_rsem, out_sem,
 ):
     ctx, hx, core = lax.axis_index("ctx"), lax.axis_index("hx"), lax.axis_index("core")
@@ -322,7 +312,7 @@
         c.wait_recv()
     outs = [
         pltpu.make_async_copy(src, dst, out_sem.at[n])
-        for n, (src, dst) in enumerate(((xs, xs_out), (gs, gs_out), (ws, ws_out), (rs, rs_out), (sts, st_out)))
+        for n, (src, dst) in enumerate(((xs, xs_out), (gs, gs_out), (ws, ws_out), (sts, st_out)))
     ]
     for c in outs:
         c.start()
@@ -372,8 +362,51 @@
             hops[0].start()
     make_ends(hx, ends.at[hx])
 
+    cum_t[...] = jnp.transpose(cum)
+    doc_col = doc_of(starts, begin + iota((BLOCK, 1), 0))
+    doc_row = doc_of(starts, begin + iota((1, BLOCK), 1))
+    ok = (iota((BLOCK, BLOCK), 0) <= iota((BLOCK, BLOCK), 1)) & (doc_col == doc_row)
+    lane = iota((BLOCK, 2 * HD), 1) < HD
+
+    def inside(group, _):
+        spread = spread_matrix(columns, core * chips + group)
+        skips = widen(jnp.broadcast_to(gains[...], (8, 128)), spread)[0:1, :]
+        wv = ws[:, cols(group, NS)]
+        rv = rs[:, cols(group, NS)]
+        scores = dot_nt(wv, rv)
+        joint = jnp.zeros((BLOCK, BLOCK), F32)
+        offset = pl.multiple_of((core * chips + group) * heads, heads)
+        rows_t = cum_t[pl.ds(offset, heads), :]
+        cols_t = jnp.transpose(jnp.concatenate([rows_t, jnp.zeros((128 - heads, BLOCK), F32)], axis=0))
+        for p in range(heads // 2):
+            at = pl.ds(pl.multiple_of(group * columns + p * 2 * HD, 2 * HD), 2 * HD)
+            xp = xs[:, at]
+            gp = gs[:, at]
+            zero = jnp.zeros_like(xp)
+            inner = skips[:, p * 2 * HD : (p + 1) * 2 * HD] * gp.astype(F32)
+            for part in range(2):
+                h = 2 * p + part
+                mine = lane if part == 0 else ~lane
+                decay = jnp.exp2(jnp.where(ok, rows_t[h : h + 1, :] - cols_t[:, h : h + 1], NEG))
+                joint += decay * dot_nt(jnp.where(mine, xp, zero), gp)
+                mixing = (scores * decay).astype(BF16)
+                inner += dot_nn(mixing, jnp.where(mine, gp, zero))
+            ix[:, at] = inner
+        low = joint.astype(BF16)
+        iw_in[:, cols(group, NS)] = dot_nn(low, rv)
+        ir_in[:, cols(group, NS)] = dot_tn(low, wv)
+        return 0
+
+    lax.fori_loop(0, chips // 2, inside, 0)
     hops[0].wait_recv()
     hops[1].start()
+    lax.fori_loop(chips // 2, chips, inside, 0)
+    more = [
+        pltpu.make_async_copy(src, dst, out_sem.at[4 + n])
+        for n, (src, dst) in enumerate(((ix, ix_out), (iw_in, iw_out), (ir_in, ir_out)))
+    ]
+    for c in more:
+        c.start()
 
     for c in end_moves:
         c.wait_recv()
@@ -460,7 +493,7 @@
         fwd[REACH - 1][part].wait_recv()
         over(part, chip_states)
     hops[REACH - 1].wait_recv()
-    for c in qg_own + outs:
+    for c in qg_own + outs + more:
         c.wait()
     for c in qg_moves:
         c.wait_recv()
@@ -468,7 +501,7 @@
         c.wait_send()
 
 
-def first_stage(lengths, slow, x, g, w, r, st, q, k, v, ag, fast, parts, cores):
+def first_stage(lengths, slow, x, g, w, r, st, q, k, v, ag, fast, gains, parts, cores):
     chips = parts // cores
     tokens = x.shape[0]
     rows = tokens * parts
@@ -482,14 +515,16 @@
     dma = pltpu.SemaphoreType.DMA
     return pl.pallas_call(
         first_kernel,
-        in_specs=[pl.BlockSpec(memory_space=pltpu.SMEM)] * 2 + [hbm] * 9 + [vmem],
-        out_specs=[hbm] * 7 + [vmem],
+        in_specs=[pl.BlockSpec(memory_space=pltpu.SMEM)] * 2 + [hbm] * 9 + [vmem] * 2,
+        out_specs=[hbm] * 9 + [vmem],
         out_shape=[
             jax.ShapeDtypeStruct((both_rows, half), BF16),
             jax.ShapeDtypeStruct((both_rows, half), BF16),
             jax.ShapeDtypeStruct((both_rows, thin), BF16),
-            jax.ShapeDtypeStruct((both_rows, thin), BF16),
             jax.ShapeDtypeStruct((both_rows, st.shape[1]), BF16),
+            jax.ShapeDtypeStruct((both_rows, half), F32),
+            jax.ShapeDtypeStruct((both_rows, thin), F32),
+            jax.ShapeDtypeStruct((both_rows, thin), F32),
             jax.ShapeDtypeStruct(((REACH + 1) * rows, 2 * DH), BF16),
             jax.ShapeDtypeStruct((rows, 2 * q.shape[1] // parts), BF16),
             jax.ShapeDtypeStruct((chips, 2 * columns, NS), BF16),
@@ -500,6 +535,10 @@
             pltpu.VMEM((both_rows, thin), BF16),
             pltpu.VMEM((both_rows, thin), BF16),
             pltpu.VMEM((both_rows, st.shape[1]), BF16),
+            pltpu.VMEM((both_rows, half), F32),
+            pltpu.VMEM((both_rows, thin), F32),
+            pltpu.VMEM((both_rows, thin), F32),
+            pltpu.VMEM((128, both_rows), F32),
             pltpu.VMEM((chips - 1, packed, NS), BF16),
             pltpu.VMEM((chips, packed, NS), BF16),
             pltpu.VMEM((2 * chips, heads, 128), F32),
@@ -518,25 +557,17 @@
             dma((chips,)),
             dma((REACH * 5,)),
             dma((REACH * 5,)),
-            dma((5,)),
+            dma((7,)),
         ],
         compiler_params=pltpu.CompilerParams(vmem_limit_bytes=60 << 20, collective_id=0, has_side_effects=True),
         cost_estimate=pl.CostEstimate(flops=2 * 10**9, bytes_accessed=16 << 20, transcendentals=10**5),
         name="first_stage",
-    )(lengths, slow, x, g, w, r, st, q, k, v, ag, fast)
-
-
-EDGES = [
-    pltpu.VMEM((BLOCK, 128), F32),
-    pltpu.VMEM((128, BLOCK), F32),
-    pltpu.VMEM((BLOCK, 128), F32),
-    pltpu.VMEM((BLOCK, 128), F32),
-]
+    )(lengths, slow, x, g, w, r, st, q, k, v, ag, fast, gains)
 
 
 def last_kernel(
-    lengths, slow, x, g, w, r, st, fast, gains, both, grad_q, out_x, out_w, out_r, out_q,
-    cum, cum_t, entering, to_end, res_x, res_w, res_r, own_sem, pair_send, pair_recv, q_send, q_recv,
+    lengths, slow, x, g, w, st, fast, inner_x, inner_w, inner_r, both, grad_q, out_x, out_w, out_r, out_q,
+    entering, to_end, res_x, res_w, res_r, own_sem, pair_send, pair_recv, q_send, q_recv,
 ):
     j = pl.program_id(0)
     ctx, hx, core = lax.axis_index("ctx"), lax.axis_index("hx"), lax.axis_index("core")
@@ -591,48 +622,19 @@
         moves, own = q_moves()
         for c in moves + [own]:
             c.start()
-        a, b, c, _ = edges(starts, begin, 0, st[...], rates_of(slow, fast, tokens * parts * lax.axis_size("ctx")))
-        cum[...] = a
-        cum_t[...] = jnp.transpose(a)
+        _, b, c, _ = edges(starts, begin, 0, st[...], rates_of(slow, fast, tokens * parts * lax.axis_size("ctx")))
         entering[...] = b
         to_end[...] = c
 
-    doc_col = doc_of(starts, begin + iota((BLOCK, 1), 0))
-    doc_row = doc_of(starts, begin + iota((1, BLOCK), 1))
-    ok = (iota((BLOCK, BLOCK), 0) <= iota((BLOCK, BLOCK), 1)) & (doc_col == doc_row)
     spread = spread_matrix(columns, group)
-    skips = widen(jnp.broadcast_to(gains[...], (8, 128)), spread)[0:1, :]
     end_wide = widen(to_end[...], spread)
     iw = (x[...].astype(F32) * end_wide).astype(BF16)
     gw = (g[...].astype(F32) * widen(entering[...], spread)).astype(BF16)
-    wv = w[...]
-    rv = r[...]
     state = both[0, 0:columns, :]
     back = both[0, columns : 2 * columns, :]
-    carried = dot_nt(wv, back)
-    scores = dot_nt(wv, rv)
-    joint = jnp.zeros((BLOCK, BLOCK), F32)
-    lane = iota((BLOCK, 2 * HD), 1) < HD
-    offset = pl.multiple_of(group * heads, heads)
-    rows_t = cum_t[pl.ds(offset, heads), :]
-    cols_all = jnp.transpose(jnp.concatenate([rows_t, jnp.zeros((128 - heads, BLOCK), F32)], axis=0))
-    for p in range(heads // 2):
-        at = slice(p * 2 * HD, (p + 1) * 2 * HD)
-        xp = x[:, at]
-        gp = g[:, at]
-        zero = jnp.zeros_like(xp)
-        inner = skips[:, at] * gp.astype(F32) + end_wide[:, at] * carried[:, at]
-        for half in range(2):
-            h = 2 * p + half
-            mine = lane if half == 0 else ~lane
-            decay = jnp.exp2(jnp.where(ok, rows_t[h : h + 1, :] - cols_all[:, h : h + 1], NEG))
-            joint += decay * dot_nt(jnp.where(mine, xp, zero), gp)
-            mixing = (scores * decay).astype(BF16)
-            inner += dot_nn(mixing, jnp.where(mine, gp, zero))
-        res_x[j, :, at] = inner.astype(BF16)
-    low = joint.astype(BF16)
-    res_w[j] = (dot_nn(low, rv) + dot_nn(iw, back)).astype(BF16)
-    res_r[j] = (dot_tn(low, wv) + dot_nn(gw, state)).astype(BF16)
+    res_x[j] = (inner_x[...] + end_wide * dot_nt(w[...], back)).astype(BF16)
+    res_w[j] = (inner_w[...] + dot_nn(iw, back)).astype(BF16)
+    res_r[j] = (inner_r[...] + dot_nn(gw, state)).astype(BF16)
 
     for n in range(chips):
 
@@ -660,7 +662,7 @@
                 c.wait_send()
 
 
-def last_stage(lengths, slow, mix, fast, gains, both, grad_q, parts, cores):
+def last_stage(lengths, slow, mix, fast, inner, both, grad_q, parts, cores):
     chips = both.shape[0]
     columns = both.shape[1] // 2
     tokens = BLOCK // cores
@@ -676,16 +678,18 @@
                 pl.BlockSpec((BLOCK, columns), lambda j, *_: (0, j)),
                 pl.BlockSpec((BLOCK, columns), lambda j, *_: (0, j)),
                 pl.BlockSpec((BLOCK, NS), lambda j, *_: (0, j)),
-                pl.BlockSpec((BLOCK, NS), lambda j, *_: (0, j)),
                 pl.BlockSpec((BLOCK, 128), lambda j, *_: (0, 0)),
                 pl.BlockSpec((1, 128), lambda j, *_: (0, 0)),
-                pl.BlockSpec((1, 128), lambda j, *_: (0, 0)),
+                pl.BlockSpec((BLOCK, columns), lambda j, *_: (0, j)),
+                pl.BlockSpec((BLOCK, NS), lambda j, *_: (0, j)),
+                pl.BlockSpec((BLOCK, NS), lambda j, *_: (0, j)),
                 pl.BlockSpec((1, 2 * columns, NS), lambda j, *_: (j, 0, 0)),
                 hbm,
             ],
             out_specs=[hbm] * 4,
-            scratch_shapes=EDGES
-            + [
+            scratch_shapes=[
+                pltpu.VMEM((BLOCK, 128), F32),
+                pltpu.VMEM((BLOCK, 128), F32),
                 pltpu.VMEM((chips, BLOCK, columns), BF16),
                 pltpu.VMEM((chips, BLOCK, NS), BF16),
                 pltpu.VMEM((chips, BLOCK, NS), BF16),
@@ -705,7 +709,7 @@
         compiler_params=pltpu.CompilerParams(vmem_limit_bytes=56 << 20, collective_id=1, has_side_effects=True),
         cost_estimate=pl.CostEstimate(flops=8 * 10**9, bytes_accessed=14 << 20, transcendentals=5 * 10**6),
         name="last_stage",
-    )(lengths, slow, *mix, fast, gains, both, grad_q)
+    )(lengths, slow, *mix, fast, *inner, both, grad_q)
 
 
 HEAD = ("hx", "core")
@@ -717,10 +721,13 @@
     slab_first = (lax.axis_index("ctx") * x.shape[0] * parts).astype(jnp.int32).reshape(1)
     fast = fast_rates.reshape(1, MH)
     gains = skip_gains.reshape(1, MH)
-    *mix, kv, qg, both = first_stage(doc_lengths, slow_heads, x, grad, w, r, steps, q, k, v, ag, fast, parts, cores)
+    *mix, kv, qg, both = first_stage(
+        doc_lengths, slow_heads, x, grad, w, r, steps, q, k, v, ag, fast, gains, parts, cores
+    )
+    mix, inner = mix[:4], mix[4:]
     both = lax.all_to_all(both, "hx", split_axis=0, concat_axis=0, tiled=True)
     grad_q = attention(qg, kv, doc_lengths, slab_first)
-    return tuple(last_stage(doc_lengths, slow_heads, mix, fast, gains, both, grad_q, parts, cores))
+    return tuple(last_stage(doc_lengths, slow_heads, mix, fast, inner, both, grad_q, parts, cores))
 
 
 def solution(mesh):

time: 152 us -> 145 us (0.954)
  the two profiles are of different devices: /device:TPU:25 before, /device:TPU:73 now
where the time goes in v4:
time: 145 us; the launch traced here: 144 us
  Pallas kernels  132 us (91%)
  local copies, waits for them, and re-layouts  6.91 us (5%)
  starting transfers between devices  3.8 us (3%)
    pallas_call x1, Pallas kernels, first_stage(): pl.pallas_call(first_kernel, in_specs=[pl.BlockSpec(memory_space=pltpu.SM...  75.5 us
    pallas_call x1, Pallas kernels, attention(): pl.pallas_call(attention_kernel, grid_spec=pltpu.PrefetchScalarGridSpec(n...  35.8 us
    pallas_call x1, Pallas kernels, last_stage(): pl.pallas_call(last_kernel, grid_spec=pltpu.PrefetchScalarGridSpec(num_sc...  21.2 us
    unnamed x12, local copies, waits for them, and re-layouts  6.91 us
    all_to_all x1, starting transfers between devices, shards(): both = lax.all_to_all(both, 'hx', split_axis=0, concat_axis=0, tiled=True)  3.8 us
  transfers between devices with their start and end apart: 1, of which 0 were waited for; matrix products, arithmetic and copies ran while one was open for 0% of the time, Pallas kernels for 25%

profile of v4, /device:TPU:73, one launch (start us, length us, event | category | flops | bytes accessed | tf_op | source)
XLA Modules:
  0.0 143.9 jit_solution(6810699720166874652)
XLA Ops:
  0.6 75.5 %first_stage.1 = (bf16[256,4096]{1,0:T(8,128)(2,1)}, bf16[256,4096]{1,0:T(8,128)(2,1)}, bf16[256,512]{1,0:T(8,128)(2,1)}, bf16[256,128]{1,0:T(8,128)(2,1)}, f32[...) custom-call(s32[16]{0:T(128)} %lengths.5, ...), custom_call_target="tpu_custom_call" | custom-call | flops 2000000000 | bytes 16777216 | tf_op jit(solution)/shard_map/first_stage/pallas_call | solution.py:516
  76.1 3.8 %all-to-all-start = ((bf16[4,2048,128]{2,1,0:T(8,128)(2,1)}), bf16[4,2048,128]{2,1,0:T(8,128)(2,1)S(1)}, u32[]{:S(2)}, u32[]{:S(2)}) async-start(bf16[4,2048,128]{2,1,0:T(8,128)(2,1)} %get-tuple-element.21), calls=%async_computation | async-start | bytes 4194304 | tf_op jit(solution)/shard_map/all_to_all | solution.py:728
  80.0 35.8 %attention.1.grad_q = bf16[1024,512]{1,0:T(8,128)(2,1)} custom-call(s32[16]{0:T(128)} %lengths.5, s32[1]{0:T(128)} %bitcast.2.first, bf16[1024,1024]{1,0:T(8,128)(2,1)} %get-tuple-element.22.qg, bf16[4096,256]{1,0:T(8,128)(2,1)} %get-tuple-element.23.kv_all), custom_call_target="tpu_custom_call" | custom-call | flops 12000000000 | bytes 6291456 | tf_op jit(solution)/shard_map/attention/pallas_call | solution.py:143
  115.8 0.0 all-to-all-done.both
  115.8 0.0 copy-start
  115.8 1.3 copy-done
  117.1 21.2 %last_stage.1 = (bf16[128,8192]{1,0:T(8,128)(2,1)}, bf16[128,1024]{1,0:T(8,128)(2,1)}, bf16[128,1024]{1,0:T(8,128)(2,1)}, bf16[128,4096]{1,0:T(8,128)(2,1)}) custom-call(s32[16]{0:T(128)} %lengths.5, s32[64]{0:T(128)} %slow.3, bf16[256,4096]{1,0:T(8,128)(2,1)} %get-tuple-element.14.x, bf16[256,4096]{1,0:T(8,128)(2,1)} %get-tuple-element.15.g, ...), custom_call_target="tpu_custom_call" | custom-call | flops 8000000000 | bytes 14680064 | tf_op jit(solution)/shard_map/last_stage/pallas_call | solution.py:672
  138.3 0.0 copy-start.3
  138.3 0.0 copy-start.2
  138.3 0.0 copy-start.1
  138.3 3.2 %copy.21 = bf16[128,8192]{1,0:T(8,128)(2,1)} copy(bf16[128,8192]{1,0:T(8,128)(2,1)} %get-tuple-element.28) | data formatting | bytes 4194304
  141.5 0.0 copy-done.3
  141.5 0.7 copy.22
  142.2 0.0 copy-done.2
  142.2 0.7 copy.23
  142.9 0.0 copy-done.1
  142.9 1.0 copy.24
Async XLA Ops:
  76.1 39.6 %all-to-all-start = ((bf16[4,2048,128]{2,1,0:T(8,128)(2,1)}), bf16[4,2048,128]{2,1,0:T(8,128)(2,1)S(1)}, u32[]{:S(2)}, u32[]{:S(2)}) async-start(bf16[4,2048,128]{2,1,0:T(8,128)(2,1)} %get-tuple-element.21), calls=%async_computation | async-start | bytes 4194304 | tf_op jit(solution)/shard_map/all_to_all | solution.py:728
  115.8 1.3 copy-start
  138.3 3.2 %copy-start.3 = (bf16[128,1024]{1,0:T(8,128)(2,1)S(1)}, bf16[128,1024]{1,0:T(8,128)(2,1)}, u32[]{:S(2)}) copy-start(bf16[128,1024]{1,0:T(8,128)(2,1)} %get-tuple-element.29) | copy-start | bytes 786436
  138.3 3.9 %copy-start.2 = (bf16[128,1024]{1,0:T(8,128)(2,1)S(1)}, bf16[128,1024]{1,0:T(8,128)(2,1)}, u32[]{:S(2)}) copy-start(bf16[128,1024]{1,0:T(8,128)(2,1)} %get-tuple-element.30) | copy-start | bytes 786436
  138.3 4.6 %copy-start.1 = (bf16[128,4096]{1,0:T(8,128)(2,1)S(1)}, bf16[128,4096]{1,0:T(8,128)(2,1)}, u32[]{:S(2)}) copy-start(bf16[128,4096]{1,0:T(8,128)(2,1)} %get-tuple-element.31) | copy-start | bytes 3145732
